TPU v7x, 256 devices: a whole 4x4x8 slice. The times are simulated.
256 devices in a mesh: lat: 16 (over z_lo, x, core), lon: 4 (over y), bin: 4 (over z_hi).
Axes of the slice: x: 4, y: 4, z: 8 (z_hi: 4, z_lo: 2; z = z_hi * 2 + z_lo), core: 2. Of those that a mesh axis runs over, the one named last changes fastest.
Arguments:
- inputs: bfloat16 [512, 1024, 128], P(('lat', 'bin'), 'lon'), may hold values from -70 to 70
- conv_one: bfloat16 [3, 3, 128, 128], replicated, may hold values from -0.1875 to 0.1875
- conv_two: bfloat16 [3, 3, 128, 128], replicated, may hold values from -0.1875 to 0.1875
- head_weight: bfloat16 [4, 128, 512], P(None, None, 'bin'), may hold values from -45.078057 to 45.078057
- targets: int32 [4, 512, 1024], P(None, 'lat', 'lon'), may hold values from 0 to 511
Outputs:
- loss_mean: float32 [], replicated
- grad_conv_one: float32 [3, 3, 128, 128], replicated
- grad_conv_two: float32 [3, 3, 128, 128], replicated
- grad_heads: float32 [4, 128, 512], P(None, None, 'bin')
All inputs are finite; a program needn't handle non-finite values.
Results may differ from a plain program's by a relative error of at most 0.0035.
The roundings to bfloat16 on the way count: a program that leaves them out, or rounds other values in their place, can miss the bound.
Values may be sent and summed in bfloat16 or wider, within the bound.
A program may use at most 64 MiB of HBM per device.

v0:
```python
import math

import jax
import jax.numpy as jnp
from jax import lax
from jax.sharding import PartitionSpec as P


def extended(shard, sides, width):
    for axis, dim in sides:
        devices, length = (lax.axis_size(axis), shard.shape[dim])
        up = [(i, (i + 1) % devices) for i in range(devices - 1)]
        down = [(j, i) for i, j in up]
        last = lax.slice_in_dim(shard, length - width, length, axis=dim)
        leading = lax.slice_in_dim(shard, 0, width, axis=dim)
        before = lax.ppermute(last, axis, up)
        after = lax.ppermute(leading, axis, down)
        shard = jnp.concatenate([before, shard, after], axis=dim)
    return shard


def merged(shard, axis, combine):
    everything = jax.tree.map(lambda part: lax.all_gather(part, axis), shard)
    leading = jax.tree.map(lambda part: part[0], everything)

    def lap(k, so_far):
        return combine(so_far, jax.tree.map(lambda part: part[k], everything))

    return lax.fori_loop(1, lax.axis_size(axis), lap, leading)


def patches(padded, grid_rows, grid_cols):
    slices = [padded[a : a + grid_rows, b : b + grid_cols] for a in range(3) for b in range(3)]
    return jnp.concatenate(slices, axis=2).reshape(grid_rows * grid_cols, -1)


def rimmed(values_in):
    return extended(values_in, ((("lat", "bin"), 0), ("lon", 1)), 1)


def softmax_join(left, right):
    highest = jnp.maximum(left[0], right[0])
    summed = left[1] * jnp.exp(left[0] - highest) + right[1] * jnp.exp(right[0] - highest)
    return (highest, summed, left[2] + right[2])


def per_device(inputs, conv_one, conv_two, head_weight, targets):
    grid_rows, grid_cols, channels = inputs.shape
    head_count = head_weight.shape[0]
    cells_all = (
        grid_rows * lax.axis_size("lat") * lax.axis_size("bin") * grid_cols * lax.axis_size("lon")
    )
    loss_scale = 1.0 / math.sqrt(head_count * cells_all)
    inner_one = patches(rimmed(inputs), grid_rows, grid_cols)
    pre_one = jnp.dot(
        inner_one, conv_one.reshape(9 * channels, channels), preferred_element_type=jnp.float32
    )
    act_one = jnp.maximum(pre_one, 0.0).astype(jnp.bfloat16)
    inner_two = patches(
        rimmed(act_one.reshape(grid_rows, grid_cols, channels)), grid_rows, grid_cols
    )
    pre_two = jnp.dot(
        inner_two, conv_two.reshape(9 * channels, channels), preferred_element_type=jnp.float32
    )
    act_two = jnp.maximum(pre_two, 0.0).astype(jnp.bfloat16)
    gathered = lax.all_gather(
        act_two.reshape(grid_rows, grid_cols, channels), "bin", axis=0, tiled=True
    )
    features = gathered.reshape(-1, channels)
    labels = targets.reshape(head_count, -1)
    first_bin = lax.axis_index("bin") * head_weight.shape[2]
    cell_count = features.shape[0]
    bin_width = head_weight.shape[2]
    block_rows = math.gcd(cell_count, 1024)
    block_count = cell_count // block_rows
    feat_blocks = features.reshape(block_count, block_rows, channels)
    label_blocks = labels.reshape(head_count, block_count, block_rows).transpose(1, 0, 2)
    columns = jnp.arange(bin_width, dtype=jnp.int32)[None, :] + first_bin

    def head_stats(inputs_now):
        feat_rows, label_rows = inputs_now
        maxima, totals, picked = ([], [], [])
        for k in range(head_count):
            logits = jnp.dot(feat_rows, head_weight[k], preferred_element_type=jnp.float32)
            highest = jnp.max(logits, axis=1)
            maxima.append(highest)
            totals.append(jnp.sum(jnp.exp(logits - highest[:, None]), axis=1))
            picked.append(
                jnp.sum(jnp.where(columns == label_rows[k][:, None], logits, 0.0), axis=1)
            )
        return (jnp.stack(maxima), jnp.stack(totals), jnp.stack(picked))

    maxima, totals, picked = lax.map(head_stats, (feat_blocks, label_blocks))
    maxima, totals, picked = merged((maxima, totals, picked), "bin", softmax_join)
    log_total = maxima + jnp.log(totals)
    loss_part = jnp.sum(log_total - picked)

    def backward(gradients, inputs_now):
        feat_rows, label_rows, total_rows = inputs_now
        hidden_back = jnp.zeros((block_rows, channels), jnp.float32)
        for k in range(head_count):
            logits = jnp.dot(feat_rows, head_weight[k], preferred_element_type=jnp.float32)
            chosen = columns == label_rows[k][:, None]
            logit_grad = (
                (jnp.exp(logits - total_rows[k][:, None]) - jnp.where(chosen, 1.0, 0.0))
                * loss_scale
            ).astype(jnp.bfloat16)
            gradients = gradients.at[k].add(
                jnp.einsum("nc,nv->cv", feat_rows, logit_grad, preferred_element_type=jnp.float32)
            )
            hidden_back = hidden_back + jnp.einsum(
                "nv,cv->nc", logit_grad, head_weight[k], preferred_element_type=jnp.float32
            )
        return (gradients, hidden_back)

    start = jnp.zeros((head_count, channels, bin_width), jnp.float32)
    head_grads, backs = lax.scan(backward, start, (feat_blocks, label_blocks, log_total))
    hidden_back = backs.reshape(cell_count, channels)
    hidden_back = lax.psum_scatter(hidden_back, "bin", scatter_dimension=0, tiled=True)
    back_two = jnp.where(pre_two > 0, hidden_back, 0.0).astype(jnp.bfloat16)
    grad_two = jnp.einsum("nk,nc->kc", inner_two, back_two, preferred_element_type=jnp.float32)
    flipped = conv_two[::-1, ::-1].transpose(0, 1, 3, 2).reshape(9 * channels, channels)
    outer_two = patches(
        rimmed(back_two.reshape(grid_rows, grid_cols, channels)), grid_rows, grid_cols
    )
    back_act = jnp.dot(outer_two, flipped, preferred_element_type=jnp.float32)
    back_one = jnp.where(pre_one > 0, back_act, 0.0).astype(jnp.bfloat16)
    grad_one = jnp.einsum("nk,nc->kc", inner_one, back_one, preferred_element_type=jnp.float32)
    grad_one, grad_two = lax.psum((grad_one, grad_two), ("lat", "lon", "bin"))
    head_grads, loss_sum = lax.psum((head_grads, loss_part), ("lat", "lon"))
    loss_mean = loss_sum / (head_count * cells_all)
    grad_conv_one = grad_one.reshape(3, 3, channels, channels)
    grad_conv_two = grad_two.reshape(3, 3, channels, channels)
    return (loss_mean, grad_conv_one, grad_conv_two, head_grads)


def solution(mesh):
    in_specs = (
        P(("lat", "bin"), "lon", None),
        P(),
        P(),
        P(None, None, "bin"),
        P(None, "lat", "lon"),
    )
    out_specs = (P(), P(), P(), P(None, None, "bin"))
    return jax.shard_map(
        per_device, mesh=mesh, in_specs=in_specs, out_specs=out_specs, check_vma=False
    )
```

profile of v0, /device:TPU:1, one launch (start us, length us, event | category | flops | bytes accessed | tf_op | source)
XLA Modules:
  0.0 1139.1 jit_solution(2076384683649284297)
XLA Ops:
  8.2 5.7 collective-permute-start
  13.9 5.5 collective-permute-start.1
  20.6 2.2 collective-permute-done.1
  22.9 3.2 collective-permute-start.2
  26.1 1.3 collective-permute-start.3
  28.7 1.7 collective-permute-done.3
  31.8 2.4 maximum_convert_fusion.1
  34.3 5.8 collective-permute-start.5
  40.1 1.9 collective-permute-start.4
  42.0 5.9 collective-permute-done.4
  47.9 1.3 collective-permute-start.7
  49.2 4.0 collective-permute-start.6
  56.0 2.2 copy-done.2
  58.2 2.5 maximum_convert_fusion
  61.0 52.8 %all-gather.5.cloned.1.call-done = bf16[32,256,128]{2,1,0:T(8,128)(2,1)} async-done(((bf16[8,256,128]{2,1,0:T(8,128)(2,1)}), bf16[32,256,128]{2,1,0:T(8,128)(2,1)}) %all-gather.5.cloned.1.call-update) | async-done | bytes 2097168 | tf_op jit(solution)/shard_map/all_gather | solution.py:66
  113.9 54.6 %while.55 = (s32[]{:T(128)}, f32[8,4,1024]{2,1,0:T(4,128)S(1)}, f32[8,4,1024]{2,1,0:T(4,128)}, f32[8,4,1024]{2,1,0:T(4,128)}, bf16[8,1024,128]{2,1,0:T(8,128)(2,...) while((s32[]{:T(128)}, f32[8,4,1024]{2,1,0:T(4,128)S(1)}, ...), condition=%wide.region_13.14_spmd.clone, body=%wide.region_0.13_spmd.clone.sunk | while | flops 137388160 | bytes 5588181 | solution.py:93
  113.9 1.2 fusion.186
  115.1 1.2 fusion.187
  116.4 1.2 fusion.188
  117.6 1.2 fusion.189
  120.7 1.2 fusion.186
  121.9 1.2 fusion.187
  123.2 1.2 fusion.188
  124.4 1.2 fusion.189
  127.5 1.2 fusion.186
  128.8 1.2 fusion.187
  130.0 1.2 fusion.188
  131.2 1.2 fusion.189
  135.6 1.2 fusion.187
  136.8 1.2 fusion.188
  138.1 1.2 fusion.189
  142.4 1.2 fusion.187
  143.6 1.2 fusion.188
  144.9 1.2 fusion.189
  149.2 1.2 fusion.187
  150.5 1.2 fusion.188
  151.7 1.2 fusion.189
  156.0 1.2 fusion.187
  157.3 1.2 fusion.188
  158.5 1.2 fusion.189
  162.9 1.2 fusion.187
  164.1 1.2 fusion.188
  165.3 1.2 fusion.189
  169.1 17.8 %all-gather = f32[32,4,1024]{2,1,0:T(4,128)S(1)} all-gather(f32[8,4,1024]{2,1,0:T(4,128)S(1)} %get-tuple-element.411), channel_id=2, replica_groups=mesh['lat'=16,'lon'=4,'bin'=4] {'bin'}, dimensions={0}, use_global_device_ids=true | all-gather | bytes 655360 | tf_op jit(solution)/shard_map/all_gather | solution.py:23
  187.0 13.6 %all-gather.1 = f32[32,4,1024]{2,1,0:T(4,128)S(1)} all-gather(f32[8,4,1024]{2,1,0:T(4,128)} %get-tuple-element.412), channel_id=3, replica_groups=mesh['lat'=16,'lon'=4,'bin'=4] {'bin'}, dimensions={0}, use_global_device_ids=true | all-gather | bytes 655360 | tf_op jit(solution)/shard_map/all_gather | solution.py:23
  200.6 13.8 %all-gather.2 = f32[32,4,1024]{2,1,0:T(4,128)S(1)} all-gather(f32[8,4,1024]{2,1,0:T(4,128)} %get-tuple-element.413), channel_id=4, replica_groups=mesh['lat'=16,'lon'=4,'bin'=4] {'bin'}, dimensions={0}, use_global_device_ids=true | all-gather | bytes 655360 | tf_op jit(solution)/shard_map/all_gather | solution.py:23
  215.2 3.5 while.54
  219.4 42.4 %while.56 = (s32[]{:T(128)}, f32[4,128,128]{2,1,0:T(8,128)S(1)}, f32[8,1024,128]{2,1,0:T(8,128)}, bf16[8,1024,128]{2,1,0:T(8,128)(2,1)S(1)}, bf16[4,128,128]{2,1...) while((s32[]{:T(128)}, f32[4,128,128]{2,1,0:T(8,128)S(1)}, ...), condition=%wide.region_19.20_spmd.clone, body=%wide.region_18.19_spmd.clone.sunk | while | flops 406257792 | bytes 9800433 | solution.py:117
  262.6 89.7 %reduce-scatter.2.cloned.1.call-done = f32[2048,128]{1,0:T(8,128)} async-done(((f32[8192,128]{1,0:T(8,128)}), f32[2048,128]{1,0:T(8,128)}) %reduce-scatter.2.cloned.1.call-update) | async-done | bytes 1048592 | tf_op jit(solution)/shard_map/reduce_scatter | solution.py:119
  352.4 1.4 select_convert_fusion
  353.8 4.5 collective-permute-start.9
  358.3 1.9 collective-permute-start.8
  360.2 4.6 fusion.126
  364.8 1.9 collective-permute-done.8
  366.7 1.3 collective-permute-start.11
  368.0 4.0 collective-permute-start.10
  374.9 2.2 copy-done.15
  377.0 8.8 fusion.101
  385.9 135.8 %psum.28 = f32[]{:T(128)} all-reduce(f32[]{:T(128)} %get-tuple-element.553), channel_id=1, replica_groups=mesh['lat'=16,'lon'=4,'bin'=4] {'lat','lon'}, use_global_device_ids=true, to_apply=%region_17.18 | all-reduce | flops 1 | bytes 8 | tf_op jit(solution)/shard_map/psum | solution.py:130
  522.3 338.1 %all-reduce.4.cloned.1.call-done = f32[4,128,128]{2,1,0:T(8,128)} async-done(((f32[4,128,128]{2,1,0:T(8,128)}), f32[4,128,128]{2,1,0:T(8,128)}) %all-reduce.4.cloned.1.call-update) | async-done | bytes 262160 | tf_op jit(solution)/shard_map/psum | solution.py:130
  860.5 265.5 %all-reduce.6.cloned.1.call-done = (f32[3,3,128,128]{3,2,1,0:T(8,128)}, f32[3,3,128,128]{3,2,1,0:T(8,128)}) async-done(((f32[3,3,128,128]{3,2,1,0:T(8,128)}, f32[3,3,128,128]{3,2,1,0:T(8,128)}), (f32[3,3,128,128]{3,2,1,0:T(8,128)}, f32[3,3,128,128]{3,2,1,0:T(8,128)})) %all-reduce.6.cloned.1.call-update) | async-done | bytes 1179664 | tf_op jit(solution)/shard_map/psum | solution.py:129
  1125.9 1.9 copy.85
  1127.8 1.9 copy.86
  1129.7 1.7 copy.87
  (270 shorter events, 79.6 us)
Async XLA Ops:
  7.2 24.6 %copy-start = (bf16[3,3,128,128]{3,2,1,0:T(8,128)(2,1)S(1)}, bf16[3,3,128,128]{3,2,1,0:T(8,128)(2,1)}, u32[]{:S(2)}) copy-start(bf16[3,3,128,128]{3,2,1,0:T(8,128)(2,1)} %param.20) | copy-start | bytes 884740
  7.2 23.7 %copy-start.5 = (bf16[8,256,128]{2,1,0:T(8,128)(2,1)S(1)}, bf16[8,256,128]{2,1,0:T(8,128)(2,1)}, u32[]{:S(2)}) copy-start(bf16[8,256,128]{2,1,0:T(8,128)(2,1)} %param.19) | copy-start | bytes 1572868
  7.2 106.7 %all-gather.5.cloned.1.call-start = ((), (), s32[]{:S(2)}) async-start(), calls=%async_computation.1 | async-start | bytes 2621440 | tf_op jit(solution)/shard_map/all_gather | solution.py:66
  8.2 11.3 collective-permute-start
  13.9 8.9 collective-permute-start.1
  22.9 4.5 collective-permute-start.2
  26.1 4.4 collective-permute-start.3
  31.8 21.5 %copy-start.6 = (bf16[8,256,1152]{2,1,0:T(8,128)(2,1)}, bf16[8,256,1152]{2,1,0:T(8,128)(2,1)S(1)}, u32[]{:S(2)}) copy-start(bf16[8,256,1152]{2,1,0:T(8,128)(2,1)S(1)} %fusion.110) | copy-start | bytes 14155780
  34.3 7.7 collective-permute-start.5
  40.1 7.8 collective-permute-start.4
  47.9 5.4 collective-permute-start.7
  49.2 4.7 collective-permute-start.6
  54.8 3.4 copy-start.11
  55.9 5.0 copy-start.14
  55.9 58.0 %copy-start.3 = (bf16[4,128,128]{2,1,0:T(8,128)(2,1)S(1)}, bf16[4,128,128]{2,1,0:T(8,128)(2,1)}, u32[]{:S(2)}) copy-start(bf16[4,128,128]{2,1,0:T(8,128)(2,1)} %param.22) | copy-start | bytes 393220
  56.0 2.2 copy-start.2
  60.8 291.6 %reduce-scatter.2.cloned.1.call-start = ((), (), s32[]{:S(2)}) async-start(), calls=%async_computation.2 | async-start | bytes 5242880 | tf_op jit(solution)/shard_map/reduce_scatter | solution.py:119
  168.5 0.7 copy-start.13
  169.1 50.3 %copy-start.1 = (bf16[8,1024,128]{2,1,0:T(8,128)(2,1)S(1)}, bf16[8,1024,128]{2,1,0:T(8,128)(2,1)}, u32[]{:S(2)}) copy-start(bf16[8,1024,128]{2,1,0:T(8,128)(2,1)} %get-tuple-element.944) | copy-start | bytes 6291460
  200.6 13.9 %copy-start.8 = (f32[32,4,1024]{2,1,0:T(4,128)}, f32[32,4,1024]{2,1,0:T(4,128)S(1)}, u32[]{:S(2)}) copy-start(f32[32,4,1024]{2,1,0:T(4,128)S(1)} %all-gather.1) | copy-start | bytes 1572868
  214.4 0.8 copy-start.9
  219.4 42.5 %copy-start.12 = (bf16[3,3,128,128]{3,2,1,0:T(8,128)(2,1)S(1)}, bf16[3,3,128,128]{3,2,1,0:T(8,128)(2,1)}, u32[]{:S(2)}) copy-start(bf16[3,3,128,128]{3,2,1,0:T(8,128)(2,1)} %param.21) | copy-start | bytes 884740
  261.8 0.7 copy-start.4
  261.8 90.6 %copy-start.7 = (f32[2048,128]{1,0:T(8,128)S(1)}, f32[2048,128]{1,0:T(8,128)}, u32[]{:S(2)}) copy-start(f32[2048,128]{1,0:T(8,128)} %get-tuple-element.613) | copy-start | bytes 3145732
  261.9 598.6 %all-reduce.4.cloned.1.call-start = ((), (), s32[]{:S(2)}) async-start(), calls=%async_computation.3 | async-start | bytes 524288 | tf_op jit(solution)/shard_map/psum | solution.py:130
  262.6 863.3 %all-reduce.6.cloned.1.call-start = ((), (), s32[]{:S(2)}) async-start(), calls=%async_computation.4 | async-start | bytes 2359296 | tf_op jit(solution)/shard_map/psum | solution.py:129
  353.8 11.1 collective-permute-start.9
  358.3 8.4 collective-permute-start.8
  366.7 5.4 collective-permute-start.11
  368.0 4.7 collective-permute-start.10
  373.8 3.3 copy-start.10
  374.8 2.2 copy-start.15
Sparse Core Ops, SparseCore 0:
  60.9 52.9 all-gather.4
  262.0 90.3 reduce-scatter.1
  355.8 504.6 all-reduce.3
  866.4 259.4 all-reduce.5
where the time goes:
time: 1140 us
  waiting for transfers between devices  759 us (67%)
  blocking collectives  181 us (16%)
  matrix products  92 us (8%)
  starting transfers between devices  40.6 us (4%)
  local copies, waits for them, and re-layouts  25.3 us (2%)
  other arithmetic  23.5 us (2%)
  between operations  16.2 us (1%)
    psum x1, waiting for transfers between devices, per_device(): head_grads, loss_sum = lax.psum((head_grads, loss_part), ('lat', 'lon'))  338 us
    psum x1, waiting for transfers between devices, per_device(): grad_one, grad_two = lax.psum((grad_one, grad_two), ('lat', 'lon', 'bin'))  265 us
    psum x1, blocking collectives, per_device(): head_grads, loss_sum = lax.psum((head_grads, loss_part), ('lat', 'lon'))  136 us
    reduce_scatter x1, waiting for transfers between devices, per_device(): lax.psum_scatter(hidden_back, 'bin', scatter_dimension=0, tiled=True)  89.7 us
    all_gather x1, waiting for transfers between devices, per_device(): lax.all_gather(act_two.reshape(grid_rows, grid_cols, channels), 'bin', ax...  52.8 us
    all_gather x3, blocking collectives, merged(): everything = jax.tree.map(lambda part: lax.all_gather(part, axis), shard)  45.3 us
    dot_general x32, matrix products, head_stats(): jnp.dot(feat_rows, head_weight[k], preferred_element_type=jnp.float32)  39.3 us
  transfers between devices with their start and end apart: 16, of which 10 were waited for; matrix products, arithmetic and copies ran while one was open for 2% of the time, Pallas kernels for 0%

commit v1 on v0

v1 whole, which is shorter than its diff:
```python
import functools
import math

import jax
import jax.numpy as jnp
from jax import lax
from jax.experimental import pallas as pl
from jax.experimental.pallas import tpu as pltpu
from jax.sharding import PartitionSpec as P

BF = jnp.bfloat16
F32 = jnp.float32
MESH = pl.DeviceIdType.MESH
CORES = 2
PLANE_X = 4


def dot(left, right, contract=((1,), (0,))):
    return lax.dot_general(left, right, (contract, ((), ())), preferred_element_type=F32)


def layout(lat, lon, bins):
    plane_x = min(PLANE_X, lat // CORES)
    return dict(nx=plane_x, nzl=lat // (CORES * plane_x), ny=lon, nzh=bins)


def plan(lat, lon, bins, rows, width, channels, heads, bin_width):
    d = layout(lat, lon, bins)
    nq, nz = d["nx"] * d["ny"], d["nzl"] * d["nzh"]
    qr = channels // nq
    pitch = width + 16
    total = bins * bin_width
    vm, dma = pltpu.VMEM, pltpu.SemaphoreType.DMA
    s = dict(
        frame=vm(((rows + 2) * pitch, channels), F32),
        px=vm(((rows + 2) * width, 3 * channels), BF),
        pa=vm(((rows + 2) * width, 3 * channels), BF),
        pg=vm(((rows + 2) * width, 3 * channels), BF),
        w_one=vm((12 * channels, 2 * channels), BF),
        w_two=vm((12 * channels, 2 * channels), BF),
        w_flip=vm((12 * channels, 2 * channels), BF),
        act_one=vm((rows, width, channels), BF),
        act_two=vm((rows, width, channels), BF),
        back_two=vm((rows + 2, width, channels), BF),
        back_one=vm((rows + 2, width, channels), BF),
        pre_one=vm((rows, width, channels), F32),
        pre_two=vm((rows, width, channels), F32),
        hw_all=vm((bins, heads, channels, bin_width), BF),
        hw_rows=vm((heads, total, channels), BF),
        hw_cols=vm((heads, channels, total), BF),
        gh_acc=vm((heads, total, channels), F32),
        loss_acc=vm((1, width), F32),
        g_acc=vm((3 * channels, 3 * channels), F32),
        col_out=vm((3, 2, rows, channels), F32),
        col_in=vm((3, 2, 3, rows, channels), F32),
        row_in=vm((3, 2, width, channels), BF),
        halo_send=dma((3, 8)),
        halo_recv=dma((3, 8)),
        hw_send=dma((2, bins)),
        hw_recv=dma((2, bins)),
    )
    shapes = dict(gh=((bins, heads // 2), (heads // 2,)), g2=((5,), (5,)), g1=((5,), (5,)))
    for name, (first, second) in shapes.items():
        tile = (qr, channels)
        s[name + "_part"] = vm((2, nq) + first + tile, BF)
        s[name + "_core"] = vm((nq,) + first + tile, BF)
        s[name + "_half"] = vm((nq,) + first + tile, BF)
        s[name + "_plane"] = vm((nq,) + first + tile, BF)
        s[name + "_sum"] = vm(first + tile, BF)
        s[name + "_ring"] = vm((nz,) + second + tile, BF)
        s[name + "_out"] = vm((2, nq) + second + tile, BF)
        s[name + "_send"] = dma((2 + 2 * nq + nz,))
        s[name + "_recv"] = dma((2 + 2 * nq + nz,))
    return s


class Place:
    def __init__(self, lat, lon, bins):
        self.__dict__.update(layout(lat, lon, bins))
        self.lat_size, self.lon_size, self.bin_size = lat, lon, bins
        self.lat, self.lon, self.bin = (lax.axis_index(a) for a in ("lat", "lon", "bin"))
        self.core = self.lat % CORES
        self.x = (self.lat // CORES) % self.nx
        self.zlo = self.lat // (CORES * self.nx)
        self.y = self.lon
        self.nq, self.nz = self.nx * self.ny, self.nzl * self.nzh
        self.z = self.bin * self.nzl + self.zlo
        self.q = self.x * self.ny + self.y
        self.row_block = self.lat * bins + self.bin
        self.row_blocks = lat * bins

    def device(self, lat=None, lon=None, bin=None):
        pick = lambda v, own: own if v is None else v
        return dict(lat=pick(lat, self.lat), lon=pick(lon, self.lon), bin=pick(bin, self.bin))

    def at(self, core=None, x=None, zlo=None):
        core = self.core if core is None else core
        x = self.x if x is None else x
        zlo = self.zlo if zlo is None else zlo
        return (zlo * self.nx + x) * CORES + core

    def partner(self):
        return self.device(lat=self.at(core=1 - self.core))

    def plane(self):
        for dx in range(self.nx):
            for dy in range(self.ny):
                if dx or dy:
                    x, y = (self.x + dx) % self.nx, (self.y + dy) % self.ny
                    yield dx * self.ny + dy, x * self.ny + y, self.device(lat=self.at(x=x), lon=y)

    def ring(self):
        for dz in range(1, self.nz):
            z = (self.z + dz) % self.nz
            zhi, zlo = z // self.nzl, z % self.nzl
            yield dz, zhi, self.device(lat=self.at(zlo=zlo), bin=zhi)

    def bins(self):
        for db in range(1, self.bin_size):
            yield db, self.device(bin=(self.bin + db) % self.bin_size)

    def neighbour(self, down, right):
        block = (self.row_block + down) % self.row_blocks
        return self.device(
            lat=block // self.bin_size, lon=(self.lon + right) % self.lon_size, bin=block % self.bin_size
        )


NEIGHBOURS = [(-1, 0), (1, 0), (0, -1), (0, 1), (-1, -1), (-1, 1), (1, -1), (1, 1)]


def enter(place):
    barrier = pltpu.get_barrier_semaphore()
    peers = [place.neighbour(*n) for n in NEIGHBOURS]
    peers += [place.partner()]
    peers += [device for _, _, device in place.plane()]
    peers += [device for _, _, device in place.ring()]
    for device in peers:
        pl.semaphore_signal(barrier, inc=1, device_id=device, device_id_type=MESH)
    pl.semaphore_wait(barrier, len(peers))


def remote(src, dst, send, recv, device):
    copy = pltpu.make_async_remote_copy(
        src_ref=src, dst_ref=dst, send_sem=send, recv_sem=recv, device_id=device, device_id_type=MESH
    )
    copy.start()
    return copy


class Halo:
    def __init__(self, k, place, s):
        self.k, self.place, self.s = k, place, s
        self.rows, self.width, _ = s["act_one"].shape
        self.pitch = self.width + 16

    def line(self, r):
        return pl.ds((r + 1) * self.pitch + 8, self.width)

    def column(self, c):
        return pl.ds(self.pitch + 8 + c, self.rows, stride=self.pitch)

    def send(self, rows_ref, top, bottom):
        k, place, s, frame = self.k, self.place, self.s, self.s["frame"]
        self.copies = []

        def go(i, src, dst, down, right):
            self.copies.append(
                remote(src, dst, s["halo_send"].at[k, i], s["halo_recv"].at[k, i], place.neighbour(down, right))
            )

        go(0, rows_ref.at[top], s["row_in"].at[k, 1], -1, 0)
        go(1, rows_ref.at[bottom], s["row_in"].at[k, 0], 1, 0)
        s["col_out"][k, 0] = frame[self.column(0), :]
        s["col_out"][k, 1] = frame[self.column(self.width - 1), :]
        for i, (down, right) in list(enumerate(NEIGHBOURS))[2:]:
            src = s["col_out"].at[k, 0 if right < 0 else 1]
            dst = s["col_in"].at[k, 1 if right < 0 else 0, 1 - down]
            go(i, src, dst, down, right)

    def receive(self):
        k, place, s, frame = self.k, self.place, self.s, self.s["frame"]
        for copy in self.copies:
            copy.wait()
        up = place.row_block > 0
        down = place.row_block < place.row_blocks - 1
        left = place.lon > 0
        right = place.lon < place.lon_size - 1
        rows, width, pitch = self.rows, self.width, self.pitch
        frame[self.line(-1), :] = jnp.where(up, s["row_in"][k, 0].astype(F32), 0.0)
        frame[self.line(rows), :] = jnp.where(down, s["row_in"][k, 1].astype(F32), 0.0)
        for side, there, c in ((0, left, -1), (1, right, width)):
            got = s["col_in"]
            frame[self.column(c), :] = jnp.where(there, got[k, side, 1], 0.0)
            frame[pl.ds(8 + c, 1), :] = jnp.where(
                there & up, got[k, side, 0, pl.ds(rows - 1, 1), :], 0.0
            )
            frame[pl.ds((rows + 1) * pitch + 8 + c, 1), :] = jnp.where(
                there & down, got[k, side, 2, pl.ds(0, 1), :], 0.0
            )


def fill_patches(frame, patches, rows, width):
    pitch = width + 16

    def body(r, carry):
        to = pl.multiple_of(r * width, width)
        for b in range(3):
            window = frame[pl.ds(r * pitch + 7 + b, width), :]
            patches[pl.ds(to, width), b * 128 : (b + 1) * 128] = window.astype(BF)
        return carry

    lax.fori_loop(0, rows + 2, body, 0)


def fill_weights(out, taps, channels):
    wide = 3 * channels
    out[pl.ds(3 * wide, wide), :channels] = jnp.zeros((wide, channels), BF)
    out[pl.ds(0, wide), channels:] = jnp.zeros((wide, channels), BF)
    for a in range(3):
        for b in range(3):
            tap = taps(a, b)
            for second in range(2):
                at = (a + second) * wide + b * channels
                out[at : at + channels, second * channels : (second + 1) * channels] = tap


def convolve(patches, weights, rows, width, finish):
    def body(p, carry):
        lines = [
            patches[pl.ds(pl.multiple_of((2 * p + a) * width, width), width), :] for a in range(4)
        ]
        both = dot(jnp.concatenate(lines, axis=1), weights[...])
        half = both.shape[1] // 2
        finish(2 * p, both[:, :half])
        finish(2 * p + 1, both[:, half:])
        return carry

    lax.fori_loop(0, rows // 2, body, 0)


def kernel_grad(patches, upstream, acc, rows, width):
    channels = upstream.shape[2]
    upstream[0] = jnp.zeros((width, channels), BF)
    upstream[rows + 1] = jnp.zeros((width, channels), BF)
    group = rows // 2
    for g in range(2):
        left = patches[pl.ds((1 + g * group) * width, group * width), :]
        right = jnp.concatenate(
            [
                jnp.concatenate([upstream[1 + g * group + r + 1 - a] for a in range(3)], axis=1)
                for r in range(group)
            ],
            axis=0,
        )
        value = dot(left, right, ((0,), (0,)))
        if g == 0:
            acc[...] = value
        else:
            acc[...] += value
    acc[:, :channels] += dot(patches[pl.ds(0, width), :], upstream[1], ((0,), (0,)))
    acc[:, 2 * channels :] += dot(
        patches[pl.ds((rows + 1) * width, width), :], upstream[rows], ((0,), (0,))
    )


def joined(tile):
    total = jnp.sum(tile, axis=0, keepdims=True)
    high = total.astype(BF).astype(F32)
    row = lax.broadcasted_iota(jnp.int32, tile.shape, 0)
    return jnp.where(row == 0, high, jnp.where(row == 1, total - high, 0.0))


class Reduce:
    def __init__(self, name, place, s, spread, extra=False):
        self.place, self.spread, self.extra = place, spread, extra
        for part in ("part", "core", "half", "plane", "sum", "ring", "out", "send", "recv"):
            setattr(self, part, s[name + "_" + part])
        self.sems = 0

    def go(self, src, dst, i, device):
        return remote(src, dst, self.send.at[i], self.recv.at[i], device)

    def rounded(self, value):
        if not self.extra:
            return value.astype(BF)
        last = jnp.where(self.place.core == 1, joined(value[4]), value[4])
        return jnp.concatenate([value[:4], last[None]], axis=0).astype(BF)

    def step0(self):
        p = self.place
        self.copies = [self.go(self.part.at[1 - p.core], self.core, 0, p.partner())]

    def step1(self):
        p = self.place
        for copy in self.copies:
            copy.wait()

        def body(i, carry):
            value = self.part[p.core, i].astype(F32) + self.core[i].astype(F32)
            self.half[i] = self.rounded(value)
            return carry

        lax.fori_loop(0, p.nq, body, 0)
        self.copies = [
            self.go(self.half.at[q], self.plane.at[d], 1 + d, device) for d, q, device in p.plane()
        ]

    def step2(self):
        p = self.place
        for copy in self.copies:
            copy.wait()
        value = self.half[p.q].astype(F32)
        for d in range(1, p.nq):
            value = value + self.plane[d].astype(F32)
        self.sum[...] = self.rounded(value)
        if self.spread:
            self.ring[p.z] = self.sum[p.bin]
        else:
            self.ring[p.z] = self.sum[...]
        self.copies = [
            self.go(self.sum.at[zhi] if self.spread else self.sum, self.ring.at[p.z], 1 + p.nq + dz, device)
            for dz, zhi, device in p.ring()
        ]

    def step3(self):
        p = self.place
        for copy in self.copies:
            copy.wait()
        value = self.ring[0].astype(F32)
        for z in range(1, p.nz):
            value = value + self.ring[z].astype(F32)
        self.out[p.core, p.q] = self.rounded(value)
        mine = self.out.at[p.core, p.q]
        base = 1 + p.nq + p.nz
        self.copies = [self.go(mine, mine, base + d, device) for d, _, device in p.plane()]

    def step4(self):
        p = self.place
        for copy in self.copies:
            copy.wait()
        mine = self.out.at[p.core]
        self.copies = [self.go(mine, mine, 1 + 2 * p.nq + p.nz, p.partner())]

    def step5(self):
        for copy in self.copies:
            copy.wait()


def pack_grad(acc, part, channels):
    qr = part.shape[-2]
    for a in range(3):
        for b in range(3):
            c, t = divmod(3 * a + b, 5)
            tap = acc[b * channels : (b + 1) * channels, a * channels : (a + 1) * channels]
            part[c, :, t] = tap.reshape(channels // qr, qr, channels).astype(BF)


def unpack_grad(out, result, channels):
    for a in range(3):
        for b in range(3):
            c, t = divmod(3 * a + b, 5)
            result[a, b] = out[c, :, t].astype(F32).reshape(channels, channels)


def turned(tile):
    return jnp.transpose(tile.astype(F32)).astype(BF)


def kernel(sizes, names, x_ref, w1_ref, w2_ref, hw_ref, tg_ref, loss_ref, g1_ref, g2_ref, gh_ref, *refs):
    lat, lon, bins, cells_all = sizes
    s = dict(zip(names, refs))
    place = Place(lat, lon, bins)
    rows, width, channels = x_ref.shape
    heads, total = s["gh_acc"].shape[:2]
    bin_width = total // bins
    frame = s["frame"]
    scale = 1.0 / math.sqrt(heads * cells_all)

    enter(place)

    halo = Halo(0, place, s)
    for r in range(rows):
        frame[halo.line(r), :] = x_ref[r].astype(F32)
    halo.send(x_ref, 0, rows - 1)

    hw_all = s["hw_all"]
    half_heads = heads // 2
    my_heads = pl.ds(place.core * half_heads, half_heads)
    hw_copies = [
        remote(
            hw_ref.at[my_heads],
            hw_all.at[place.bin, my_heads],
            s["hw_send"].at[0, db],
            s["hw_recv"].at[0, db],
            device,
        )
        for db, device in place.bins()
    ]
    hw_all[place.bin] = hw_ref[...]
    fill_weights(s["w_one"], lambda a, b: w1_ref[a, b], channels)
    fill_weights(s["w_two"], lambda a, b: w2_ref[a, b], channels)
    fill_weights(s["w_flip"], lambda a, b: turned(w2_ref[2 - a, 2 - b]), channels)

    halo.receive()
    fill_patches(frame, s["px"], rows, width)

    def finish_one(r, value):
        s["pre_one"][r] = value
        act = jnp.maximum(value, 0.0).astype(BF)
        s["act_one"][r] = act
        frame[pl.ds(pl.multiple_of((r + 1) * halo.pitch + 8, 8), width), :] = act.astype(F32)

    convolve(s["px"], s["w_one"], rows, width, finish_one)
    halo = Halo(1, place, s)
    halo.send(s["act_one"], 0, rows - 1)

    for copy in hw_copies:
        copy.wait()
    hw_copies = []
    for db in range(1, bins):
        there = hw_all.at[(place.bin + db) % bins, my_heads]
        hw_copies.append(
            remote(there, there, s["hw_send"].at[1, db], s["hw_recv"].at[1, db], place.partner())
        )

    halo.receive()
    fill_patches(frame, s["pa"], rows, width)

    def finish_two(r, value):
        s["pre_two"][r] = value
        s["act_two"][r] = jnp.maximum(value, 0.0).astype(BF)

    convolve(s["pa"], s["w_two"], rows, width, finish_two)

    for copy in hw_copies:
        copy.wait()
    hw_rows, hw_cols, gh_acc = s["hw_rows"], s["hw_cols"], s["gh_acc"]
    for b in range(bins):
        for k in range(heads):
            tile = hw_all[b, k]
            hw_cols[k, :, b * bin_width : (b + 1) * bin_width] = tile
            hw_rows[k, b * bin_width : (b + 1) * bin_width, :] = turned(tile)
    gh_acc[...] = jnp.zeros_like(gh_acc)
    s["loss_acc"][...] = jnp.zeros_like(s["loss_acc"])
    first_row = place.bin * rows

    def heads_body(r, carry):
        feat = s["act_two"][r]
        feat_t = turned(feat)
        back = jnp.zeros((channels, width), F32)
        loss = s["loss_acc"][...]
        for k in range(heads):
            logits = dot(hw_rows[k], feat_t)
            highest = jnp.max(logits, axis=0, keepdims=True)
            raised = jnp.exp(logits - highest)
            summed = jnp.sum(raised, axis=0, keepdims=True)
            label = tg_ref[k, pl.ds(first_row + r, 1), :]
            chosen = lax.broadcasted_iota(jnp.int32, logits.shape, 0) == label
            picked = jnp.sum(jnp.where(chosen, logits, 0.0), axis=0, keepdims=True)
            loss = loss + (highest + jnp.log(summed) - picked)
            grad = (raised * (scale / summed) - jnp.where(chosen, scale, 0.0)).astype(BF)
            gh_acc[k] += dot(grad, feat)
            back = back + dot(hw_cols[k], grad)
        s["loss_acc"][...] = loss
        hidden = jnp.where(s["pre_two"][r] > 0, jnp.transpose(back), 0.0)
        s["back_two"][r + 1] = hidden.astype(BF)
        frame[pl.ds(pl.multiple_of((r + 1) * halo.pitch + 8, 8), width), :] = hidden.astype(BF).astype(F32)
        return carry

    lax.fori_loop(0, rows, heads_body, 0)
    halo = Halo(2, place, s)
    halo.send(s["back_two"], 1, rows)

    gh = Reduce("gh", place, s, True)
    g2 = Reduce("g2", place, s, False, extra=True)
    g1 = Reduce("g1", place, s, False)
    qr = gh.part.shape[-2]
    for k in range(heads):
        c, kk = divmod(k, half_heads)
        for b in range(bins):
            block = gh_acc[k, b * bin_width : (b + 1) * bin_width, :]
            gh.part[c, :, b, kk] = block.reshape(bin_width // qr, qr, channels).astype(BF)
    gh.step0()

    kernel_grad(s["pa"], s["back_two"], s["g_acc"], rows, width)
    pack_grad(s["g_acc"], g2.part, channels)
    loss = s["loss_acc"][...]
    lanes = loss[:, :128]
    for i in range(1, width // 128):
        lanes = lanes + loss[:, i * 128 : (i + 1) * 128]
    row = lax.broadcasted_iota(jnp.int32, (qr, 128), 0)
    loss_tile = joined(jnp.where(row == 0, lanes, 0.0)).astype(BF)
    for q in range(place.nq):
        g2.part[1, q, 4] = loss_tile
        g1.part[1, q, 4] = jnp.zeros((qr, channels), BF)
    g2.step0()

    halo.receive()
    fill_patches(frame, s["pg"], rows, width)
    gh.step1()

    def finish_back(r, value):
        s["back_one"][r + 1] = jnp.where(s["pre_one"][r] > 0, value, 0.0).astype(BF)

    convolve(s["pg"], s["w_flip"], rows, width, finish_back)
    g2.step1()
    kernel_grad(s["px"], s["back_one"], s["g_acc"], rows, width)
    pack_grad(s["g_acc"], g1.part, channels)
    g1.step0()
    gh.step2()
    g1.step1()
    g2.step2()
    gh.step3()
    g1.step2()
    g2.step3()
    g1.step3()
    gh.step4()
    g2.step4()
    gh.step5()
    for k in range(heads):
        c, kk = divmod(k, half_heads)
        gh_ref[k] = jnp.transpose(gh.out[c, :, kk].astype(F32).reshape(bin_width, channels))
    g2.step5()
    unpack_grad(g2.out, g2_ref, channels)
    whole = jnp.sum(g2.out[1, 0, 4].astype(F32), axis=0, keepdims=True)
    loss_ref[...] = jnp.sum(whole, axis=1, keepdims=True) * (1.0 / (heads * cells_all))
    g1.step4()
    g1.step5()
    unpack_grad(g1.out, g1_ref, channels)


def per_device(inputs, conv_one, conv_two, head_weight, targets):
    rows, width, channels = inputs.shape
    heads, _, bin_width = head_weight.shape
    lat, lon, bins = (lax.axis_size(a) for a in ("lat", "lon", "bin"))
    cells_all = rows * lat * bins * width * lon
    scratch = plan(lat, lon, bins, rows, width, channels, heads, bin_width)
    vmem = pl.BlockSpec(memory_space=pltpu.VMEM)
    loss, g1, g2, gh = pl.pallas_call(
        functools.partial(kernel, (lat, lon, bins, cells_all), tuple(scratch)),
        out_shape=[
            jax.ShapeDtypeStruct((1, 1), F32),
            jax.ShapeDtypeStruct(conv_one.shape, F32),
            jax.ShapeDtypeStruct(conv_two.shape, F32),
            jax.ShapeDtypeStruct(head_weight.shape, F32),
        ],
        in_specs=[vmem] * 5,
        out_specs=[vmem] * 4,
        scratch_shapes=list(scratch.values()),
        compiler_params=pltpu.CompilerParams(
            collective_id=0, has_side_effects=True, vmem_limit_bytes=56 << 20
        ),
    )(inputs, conv_one, conv_two, head_weight, targets)
    return (loss.reshape(()), g1, g2, gh)


def solution(mesh):
    in_specs = (
        P(("lat", "bin"), "lon", None),
        P(),
        P(),
        P(None, None, "bin"),
        P(None, "lat", "lon"),
    )
    out_specs = (P(), P(), P(), P(None, None, "bin"))
    return jax.shard_map(
        per_device, mesh=mesh, in_specs=in_specs, out_specs=out_specs, check_vma=False
    )
```

time: 1140 us -> 89.1 us (0.08)
  waiting for transfers between devices: 759 us -> 0 us
  blocking collectives: 181 us -> 0 us
  matrix products: 92 us -> 0 us
  Pallas kernels: 0 us -> 82.8 us
  starting transfers between devices: 40.6 us -> 0 us
  other arithmetic: 23.5 us -> 0 us
  local copies, waits for them, and re-layouts: 25.3 us -> 3.78 us
  between operations: 16.2 us -> 2.4 us
    psum x2 -> x0, waiting for transfers between devices: 604 us -> none  [the longest x1 338 us: per_device(): head_grads, loss_sum = lax.psum((head_grads, loss_part), ('lat', 'lon'))]
    psum x1 -> x0, blocking collectives: 136 us -> none  [per_device(): head_grads, loss_sum = lax.psum((head_grads, loss_part), ('lat', 'lon'))]
    dot_general x132 -> x0, matrix products: 92 us -> none  [the longest x32 39.3 us: head_stats(): jnp.dot(feat_rows, head_weight[k], preferred_element_type=jnp.float32)]
    reduce_scatter x1 -> x0, waiting for transfers between devices: 89.7 us -> none  [per_device(): lax.psum_scatter(hidden_back, 'bin', scatter_dimension=0, tiled=True)]
    pallas_call x0 -> x1, Pallas kernels: none -> 82.8 us  [per_device(): pl.pallas_call(functools.partial(kernel, (lat, lon, bins, cells_all), tup...]
    all_gather x1 -> x0, waiting for transfers between devices: 52.8 us -> none  [per_device(): lax.all_gather(act_two.reshape(grid_rows, grid_cols, channels), 'bin', ax...]
    all_gather x3 -> x0, blocking collectives: 45.3 us -> none  [merged(): everything = jax.tree.map(lambda part: lax.all_gather(part, axis), shard)]
    ppermute x12 -> x0, starting transfers between devices: 40.4 us -> none  [the longest x6 20.7 us: extended(): before = lax.ppermute(last, axis, up)]
  transfers between devices with their start and end apart: 16 -> 0, of which waited for: 10 -> 0; matrix products, arithmetic and copies ran while one was open for 2% -> 0% of each run, Pallas kernels for 0% -> 0%
where the time goes in v1:
time: 89.1 us; the launch traced here: 88.9 us
  Pallas kernels  82.8 us (93%)
  local copies, waits for them, and re-layouts  3.78 us (4%)
  between operations  2.4 us (3%)
    pallas_call x1, Pallas kernels, per_device(): pl.pallas_call(functools.partial(kernel, (lat, lon, bins, cells_all), tup...  82.8 us
    unnamed x7, local copies, waits for them, and re-layouts  3.78 us

profile of v1, /device:TPU:1, one launch (start us, length us, event | category | flops | bytes accessed | tf_op | source)
XLA Modules:
  0.0 88.9 jit_solution(16958669372382001221)
XLA Ops:
  0.6 82.8 %shard_map.84 = (f32[1,1]{1,0:T(1,128)}, f32[3,3,128,128]{3,2,1,0:T(8,128)}, f32[3,3,128,128]{3,2,1,0:T(8,128)}, f32[4,128,128]{2,1,0:T(8,128)}) custom-call(bf16[8,256,128]{2,1,0:T(8,128)(2,1)} %x_ref.1, bf16[3,3,128,128]{3,2,1,0:T(8,128)(2,1)} %w1_ref.1, bf16[3,3,128,128]{3,2,1,0:T(8,128)(2,1)} %w2_ref.1, bf16[4,128,128]{2,1,0:T(8,128)(2,1)} %hw_ref.1, ...), custom_call_target="tpu_custom_call" | custom-call | tf_op jit(solution)/shard_map/pallas_call | solution.py:540
  84.0 0.0 copy-start
  84.0 2.0 %copy.14 = f32[3,3,128,128]{3,2,1,0:T(8,128)} copy(f32[3,3,128,128]{3,2,1,0:T(8,128)} %get-tuple-element.17) | data formatting | bytes 1179648
  86.0 0.0 copy-done
  86.0 0.0 copy-start.1
  86.0 0.8 copy.15
  86.8 0.3 copy-done.1
  87.1 0.7 copy.16
Async XLA Ops:
  84.0 2.0 %copy-start = (f32[3,3,128,128]{3,2,1,0:T(8,128)S(1)}, f32[3,3,128,128]{3,2,1,0:T(8,128)}, u32[]{:S(2)}) copy-start(f32[3,3,128,128]{3,2,1,0:T(8,128)} %get-tuple-element.18) | copy-start | bytes 1769476
  86.0 1.1 %copy-start.1 = (f32[4,128,128]{2,1,0:T(8,128)S(1)}, f32[4,128,128]{2,1,0:T(8,128)}, u32[]{:S(2)}) copy-start(f32[4,128,128]{2,1,0:T(8,128)} %get-tuple-element.19) | copy-start | bytes 786436

commit v2 on v1

--- a/solution.py
+++ b/solution.py
@@ -48,10 +48,16 @@
         hw_all=vm((bins, heads, channels, bin_width), BF),
         hw_rows=vm((heads, total, channels), BF),
         hw_cols=vm((heads, channels, total), BF),
-        gh_acc=vm((heads, total, channels), F32),
+        head_grad=vm((rows, heads, total, width), BF),
+        x=vm((rows, width, channels), BF),
+        w1=vm((3, 3, channels, channels), BF),
+        w2=vm((3, 3, channels, channels), BF),
+        tg=vm((heads, rows, width), jnp.int32),
+        load=dma((5,)),
+        store=dma((6,)),
         loss_acc=vm((1, width), F32),
         g_acc=vm((3 * channels, 3 * channels), F32),
-        col_out=vm((3, 2, rows, channels), F32),
+        col_out=vm((3, 2, 2, rows, channels), F32),
         col_in=vm((3, 2, 3, rows, channels), F32),
         row_in=vm((3, 2, width, channels), BF),
         halo_send=dma((3, 8)),
@@ -137,7 +143,7 @@
     peers += [device for _, _, device in place.ring()]
     for device in peers:
         pl.semaphore_signal(barrier, inc=1, device_id=device, device_id_type=MESH)
-    pl.semaphore_wait(barrier, len(peers))
+    return len(peers)
 
 
 def remote(src, dst, send, recv, device):
@@ -153,45 +159,58 @@
         self.k, self.place, self.s = k, place, s
         self.rows, self.width, _ = s["act_one"].shape
         self.pitch = self.width + 16
+        self.copies = {}
 
     def line(self, r):
-        return pl.ds((r + 1) * self.pitch + 8, self.width)
+        start = (r + 1) * self.pitch + 8
+        return pl.ds(start if isinstance(r, int) else pl.multiple_of(start, 8), self.width)
 
     def column(self, c):
         return pl.ds(self.pitch + 8 + c, self.rows, stride=self.pitch)
 
-    def send(self, rows_ref, top, bottom):
+    def go(self, i, src, dst):
+        k, s = self.k, self.s
+        self.copies[i] = remote(
+            src, dst, s["halo_send"].at[k, i], s["halo_recv"].at[k, i], self.place.neighbour(*NEIGHBOURS[i])
+        )
+
+    def send_rows(self, top, bottom):
+        self.go(0, top, self.s["row_in"].at[self.k, 1])
+        self.go(1, bottom, self.s["row_in"].at[self.k, 0])
+
+    def send_columns(self, which, use):
+        k, s, frame = self.k, self.s, self.s["frame"]
+        s["col_out"][k, which, 0] = frame[self.column(0), :]
+        s["col_out"][k, which, 1] = frame[self.column(self.width - 1), :]
+        for i in use:
+            down, right = NEIGHBOURS[i]
+            src = s["col_out"].at[k, which, 0 if right < 0 else 1]
+            self.go(i, src, s["col_in"].at[k, 1 if right < 0 else 0, 1 - down])
+
+    def send_sides(self):
+        self.send_columns(0, (2, 3))
+
+    def send_corners(self):
+        self.send_columns(1, (4, 5, 6, 7))
+
+    def receive_sides(self):
         k, place, s, frame = self.k, self.place, self.s, self.s["frame"]
-        self.copies = []
-
-        def go(i, src, dst, down, right):
-            self.copies.append(
-                remote(src, dst, s["halo_send"].at[k, i], s["halo_recv"].at[k, i], place.neighbour(down, right))
-            )
-
-        go(0, rows_ref.at[top], s["row_in"].at[k, 1], -1, 0)
-        go(1, rows_ref.at[bottom], s["row_in"].at[k, 0], 1, 0)
-        s["col_out"][k, 0] = frame[self.column(0), :]
-        s["col_out"][k, 1] = frame[self.column(self.width - 1), :]
-        for i, (down, right) in list(enumerate(NEIGHBOURS))[2:]:
-            src = s["col_out"].at[k, 0 if right < 0 else 1]
-            dst = s["col_in"].at[k, 1 if right < 0 else 0, 1 - down]
-            go(i, src, dst, down, right)
-
-    def receive(self):
+        for i in (2, 3):
+            self.copies[i].wait()
+        for side, there, c in ((0, place.lon > 0, -1), (1, place.lon < place.lon_size - 1, self.width)):
+            frame[self.column(c), :] = jnp.where(there, s["col_in"][k, side, 1], 0.0)
+
+    def receive_rest(self):
         k, place, s, frame = self.k, self.place, self.s, self.s["frame"]
-        for copy in self.copies:
-            copy.wait()
+        for i in (0, 1, 4, 5, 6, 7):
+            self.copies[i].wait()
+        rows, width, pitch = self.rows, self.width, self.pitch
         up = place.row_block > 0
         down = place.row_block < place.row_blocks - 1
-        left = place.lon > 0
-        right = place.lon < place.lon_size - 1
-        rows, width, pitch = self.rows, self.width, self.pitch
         frame[self.line(-1), :] = jnp.where(up, s["row_in"][k, 0].astype(F32), 0.0)
         frame[self.line(rows), :] = jnp.where(down, s["row_in"][k, 1].astype(F32), 0.0)
-        for side, there, c in ((0, left, -1), (1, right, width)):
+        for side, there, c in ((0, place.lon > 0, -1), (1, place.lon < place.lon_size - 1, width)):
             got = s["col_in"]
-            frame[self.column(c), :] = jnp.where(there, got[k, side, 1], 0.0)
             frame[pl.ds(8 + c, 1), :] = jnp.where(
                 there & up, got[k, side, 0, pl.ds(rows - 1, 1), :], 0.0
             )
@@ -200,17 +219,27 @@
             )
 
 
-def fill_patches(frame, patches, rows, width):
+def fill_patches(frame, patches, first, count, step, width):
     pitch = width + 16
 
-    def body(r, carry):
+    def body(i, carry):
+        r = first + i * step
         to = pl.multiple_of(r * width, width)
         for b in range(3):
             window = frame[pl.ds(r * pitch + 7 + b, width), :]
             patches[pl.ds(to, width), b * 128 : (b + 1) * 128] = window.astype(BF)
         return carry
 
-    lax.fori_loop(0, rows + 2, body, 0)
+    lax.fori_loop(0, count, body, 0)
+
+
+def fix_patches(frame, patches, rows, width):
+    pitch = width + 16
+    for r in range(1, rows + 1):
+        patches[pl.ds(r * width, 16), :128] = frame[pl.ds(r * pitch + 7, 16), :].astype(BF)
+        patches[pl.ds((r + 1) * width - 16, 16), 256:] = frame[
+            pl.ds(r * pitch + width - 7, 16), :
+        ].astype(BF)
 
 
 def fill_weights(out, taps, channels):
@@ -225,18 +254,29 @@
                 out[at : at + channels, second * channels : (second + 1) * channels] = tap
 
 
-def convolve(patches, weights, rows, width, finish):
+def convolve(patches, weights, first, pairs, step, width, finish):
     def body(p, carry):
-        lines = [
-            patches[pl.ds(pl.multiple_of((2 * p + a) * width, width), width), :] for a in range(4)
-        ]
+        r = first + p * step
+        lines = [patches[pl.ds(pl.multiple_of((r + a) * width, width), width), :] for a in range(4)]
         both = dot(jnp.concatenate(lines, axis=1), weights[...])
         half = both.shape[1] // 2
-        finish(2 * p, both[:, :half])
-        finish(2 * p + 1, both[:, half:])
+        finish(r, both[:, :half])
+        finish(r + 1, both[:, half:])
         return carry
 
-    lax.fori_loop(0, rows // 2, body, 0)
+    lax.fori_loop(0, pairs, body, 0)
+
+
+def convolve_outer(patches, weights, rows, width, finish):
+    wide, half = patches.shape[1], weights.shape[1] // 2
+
+    def body(p, carry):
+        r = p * (rows - 1)
+        lines = [patches[pl.ds(pl.multiple_of((r + a) * width, width), width), :] for a in range(3)]
+        finish(r, dot(jnp.concatenate(lines, axis=1), weights[: 3 * wide, :half]))
+        return carry
+
+    lax.fori_loop(0, 2, body, 0)
 
 
 def kernel_grad(patches, upstream, acc, rows, width):
@@ -367,25 +407,34 @@
     return jnp.transpose(tile.astype(F32)).astype(BF)
 
 
-def kernel(sizes, names, x_ref, w1_ref, w2_ref, hw_ref, tg_ref, loss_ref, g1_ref, g2_ref, gh_ref, *refs):
+def load(src, dst, sem):
+    copy = pltpu.make_async_copy(src, dst, sem)
+    copy.start()
+    return copy
+
+
+def kernel(sizes, names, x_ref, w1_ref, w2_ref, hw_ref, tg_ref, g1_ref, g2_ref, gh_ref, *refs):
     lat, lon, bins, cells_all = sizes
     s = dict(zip(names, refs))
     place = Place(lat, lon, bins)
     rows, width, channels = x_ref.shape
-    heads, total = s["gh_acc"].shape[:2]
+    heads, total, _ = s["hw_rows"].shape
     bin_width = total // bins
-    frame = s["frame"]
+    half_heads = heads // 2
+    frame, hw_all = s["frame"], s["hw_all"]
     scale = 1.0 / math.sqrt(heads * cells_all)
 
-    enter(place)
+    peers = enter(place)
+    loads = [
+        load(x_ref, s["x"], s["load"].at[0]),
+        load(w1_ref, s["w1"], s["load"].at[1]),
+        load(w2_ref, s["w2"], s["load"].at[2]),
+        load(hw_ref, hw_all.at[place.bin], s["load"].at[3]),
+        load(tg_ref.at[:, pl.ds(place.bin * rows, rows), :], s["tg"], s["load"].at[4]),
+    ]
+    pl.semaphore_wait(pltpu.get_barrier_semaphore(), peers)
 
     halo = Halo(0, place, s)
-    for r in range(rows):
-        frame[halo.line(r), :] = x_ref[r].astype(F32)
-    halo.send(x_ref, 0, rows - 1)
-
-    hw_all = s["hw_all"]
-    half_heads = heads // 2
     my_heads = pl.ds(place.core * half_heads, half_heads)
     hw_copies = [
         remote(
@@ -397,24 +446,37 @@
         )
         for db, device in place.bins()
     ]
-    hw_all[place.bin] = hw_ref[...]
-    fill_weights(s["w_one"], lambda a, b: w1_ref[a, b], channels)
-    fill_weights(s["w_two"], lambda a, b: w2_ref[a, b], channels)
-    fill_weights(s["w_flip"], lambda a, b: turned(w2_ref[2 - a, 2 - b]), channels)
-
-    halo.receive()
-    fill_patches(frame, s["px"], rows, width)
+    halo.send_rows(x_ref.at[0], x_ref.at[rows - 1])
+    loads[0].wait()
+    for r in range(rows):
+        frame[halo.line(r), :] = s["x"][r].astype(F32)
+    halo.send_sides()
+    halo.send_corners()
+
+    fill_patches(frame, s["px"], 1, rows, 1, width)
+    loads[1].wait()
+    fill_weights(s["w_one"], lambda a, b: s["w1"][a, b], channels)
+    halo.receive_sides()
+    fix_patches(frame, s["px"], rows, width)
 
     def finish_one(r, value):
         s["pre_one"][r] = value
         act = jnp.maximum(value, 0.0).astype(BF)
         s["act_one"][r] = act
-        frame[pl.ds(pl.multiple_of((r + 1) * halo.pitch + 8, 8), width), :] = act.astype(F32)
-
-    convolve(s["px"], s["w_one"], rows, width, finish_one)
+        frame[halo.line(r), :] = act.astype(F32)
+
+    convolve(s["px"], s["w_one"], 1, (rows - 2) // 2, 2, width, finish_one)
+    halo.receive_rest()
+    fill_patches(frame, s["px"], 0, 2, rows + 1, width)
+    convolve_outer(s["px"], s["w_one"], rows, width, finish_one)
     halo = Halo(1, place, s)
-    halo.send(s["act_one"], 0, rows - 1)
-
+    halo.send_sides()
+    halo.send_rows(s["act_one"].at[0], s["act_one"].at[rows - 1])
+    halo.send_corners()
+
+    fill_patches(frame, s["pa"], 1, rows, 1, width)
+    loads[2].wait()
+    fill_weights(s["w_two"], lambda a, b: s["w2"][a, b], channels)
     for copy in hw_copies:
         copy.wait()
     hw_copies = []
@@ -423,64 +485,75 @@
         hw_copies.append(
             remote(there, there, s["hw_send"].at[1, db], s["hw_recv"].at[1, db], place.partner())
         )
-
-    halo.receive()
-    fill_patches(frame, s["pa"], rows, width)
+    halo.receive_sides()
+    fix_patches(frame, s["pa"], rows, width)
 
     def finish_two(r, value):
         s["pre_two"][r] = value
         s["act_two"][r] = jnp.maximum(value, 0.0).astype(BF)
 
-    convolve(s["pa"], s["w_two"], rows, width, finish_two)
-
-    for copy in hw_copies:
+    convolve(s["pa"], s["w_two"], 2, (rows - 4) // 2, 2, width, finish_two)
+
+    for copy in loads[3:] + hw_copies:
         copy.wait()
-    hw_rows, hw_cols, gh_acc = s["hw_rows"], s["hw_cols"], s["gh_acc"]
+    hw_rows, hw_cols = s["hw_rows"], s["hw_cols"]
     for b in range(bins):
         for k in range(heads):
             tile = hw_all[b, k]
             hw_cols[k, :, b * bin_width : (b + 1) * bin_width] = tile
             hw_rows[k, b * bin_width : (b + 1) * bin_width, :] = turned(tile)
-    gh_acc[...] = jnp.zeros_like(gh_acc)
     s["loss_acc"][...] = jnp.zeros_like(s["loss_acc"])
-    first_row = place.bin * rows
-
-    def heads_body(r, carry):
-        feat = s["act_two"][r]
-        feat_t = turned(feat)
+    last_halo = Halo(2, place, s)
+
+    def heads_body(i, carry):
+        r = (i + 2) % rows
+
+        feat_t = turned(s["act_two"][r])
         back = jnp.zeros((channels, width), F32)
         loss = s["loss_acc"][...]
+        eight = lax.broadcasted_iota(jnp.int32, (8, width), 0)
+        group = lax.broadcasted_iota(jnp.int32, (total // 8, 8, width), 0)
         for k in range(heads):
-            logits = dot(hw_rows[k], feat_t)
-            highest = jnp.max(logits, axis=0, keepdims=True)
-            raised = jnp.exp(logits - highest)
-            summed = jnp.sum(raised, axis=0, keepdims=True)
-            label = tg_ref[k, pl.ds(first_row + r, 1), :]
-            chosen = lax.broadcasted_iota(jnp.int32, logits.shape, 0) == label
-            picked = jnp.sum(jnp.where(chosen, logits, 0.0), axis=0, keepdims=True)
+            logits = dot(hw_rows[k], feat_t).reshape(total // 8, 8, width)
+            highest = jnp.max(jnp.max(logits, axis=0), axis=0, keepdims=True)
+            raised = jnp.exp(logits - highest[None])
+            summed = jnp.sum(jnp.sum(raised, axis=0), axis=0, keepdims=True)
+            label = s["tg"][k, pl.ds(r, 1), :] - eight
+            chosen = group * 8 == label[None]
+            picked = jnp.sum(jnp.sum(jnp.where(chosen, logits, 0.0), axis=0), axis=0, keepdims=True)
             loss = loss + (highest + jnp.log(summed) - picked)
-            grad = (raised * (scale / summed) - jnp.where(chosen, scale, 0.0)).astype(BF)
-            gh_acc[k] += dot(grad, feat)
+            value = raised * (scale / summed)[None]
+            grad = jnp.where(chosen, value - scale, value).reshape(total, width).astype(BF)
+            s["head_grad"][r, k] = grad
             back = back + dot(hw_cols[k], grad)
         s["loss_acc"][...] = loss
-        hidden = jnp.where(s["pre_two"][r] > 0, jnp.transpose(back), 0.0)
-        s["back_two"][r + 1] = hidden.astype(BF)
-        frame[pl.ds(pl.multiple_of((r + 1) * halo.pitch + 8, 8), width), :] = hidden.astype(BF).astype(F32)
+        hidden = jnp.where(s["pre_two"][r] > 0, jnp.transpose(back), 0.0).astype(BF)
+        s["back_two"][r + 1] = hidden
+        frame[halo.line(r), :] = hidden.astype(F32)
         return carry
 
-    lax.fori_loop(0, rows, heads_body, 0)
-    halo = Halo(2, place, s)
-    halo.send(s["back_two"], 1, rows)
+    lax.fori_loop(0, rows - 4, heads_body, 0)
+    halo.receive_rest()
+    fill_patches(frame, s["pa"], 0, 2, rows + 1, width)
+    convolve(s["pa"], s["w_two"], 0, 2, rows - 2, width, finish_two)
+    lax.fori_loop(rows - 4, rows - 1, heads_body, 0)
+    last_halo.send_rows(s["back_two"].at[1], s["back_two"].at[rows])
+    last_halo.send_corners()
+    lax.fori_loop(rows - 1, rows, heads_body, 0)
+    last_halo.send_sides()
+    halo = last_halo
 
     gh = Reduce("gh", place, s, True)
     g2 = Reduce("g2", place, s, False, extra=True)
     g1 = Reduce("g1", place, s, False)
     qr = gh.part.shape[-2]
+    feats = s["act_two"][...].reshape(rows * width, channels)
     for k in range(heads):
         c, kk = divmod(k, half_heads)
+        grads = jnp.concatenate([s["head_grad"][r, k] for r in range(rows)], axis=1)
+        value = dot(grads, feats).reshape(bins, bin_width // qr, qr, channels)
         for b in range(bins):
-            block = gh_acc[k, b * bin_width : (b + 1) * bin_width, :]
-            gh.part[c, :, b, kk] = block.reshape(bin_width // qr, qr, channels).astype(BF)
+            gh.part[c, :, b, kk] = value[b].astype(BF)
     gh.step0()
 
     kernel_grad(s["pa"], s["back_two"], s["g_acc"], rows, width)
@@ -496,14 +569,18 @@
         g1.part[1, q, 4] = jnp.zeros((qr, channels), BF)
     g2.step0()
 
-    halo.receive()
-    fill_patches(frame, s["pg"], rows, width)
+    fill_weights(s["w_flip"], lambda a, b: turned(s["w2"][2 - a, 2 - b]), channels)
+    fill_patches(frame, s["pg"], 1, rows, 1, width)
     gh.step1()
+    halo.receive_sides()
+    fix_patches(frame, s["pg"], rows, width)
+    halo.receive_rest()
+    fill_patches(frame, s["pg"], 0, 2, rows + 1, width)
 
     def finish_back(r, value):
         s["back_one"][r + 1] = jnp.where(s["pre_one"][r] > 0, value, 0.0).astype(BF)
 
-    convolve(s["pg"], s["w_flip"], rows, width, finish_back)
+    convolve(s["pg"], s["w_flip"], 0, rows // 2, 2, width, finish_back)
     g2.step1()
     kernel_grad(s["px"], s["back_one"], s["g_acc"], rows, width)
     pack_grad(s["g_acc"], g1.part, channels)
@@ -518,16 +595,27 @@
     gh.step4()
     g2.step4()
     gh.step5()
+    stores = [load(gh.out, gh_ref, s["store"].at[0])]
+    g2.step5()
+    stores.append(load(g2.out, g2_ref, s["store"].at[1]))
+    g1.step4()
+    stores.append(load(g1.out.at[place.core], g1_ref.at[place.core], s["store"].at[2]))
+    g1.step5()
+    other = 1 - place.core
+    stores.append(load(g1.out.at[other], g1_ref.at[other], s["store"].at[3]))
+    for copy in stores:
+        copy.wait()
+
+
+def unpack(count, g1_in, g2_in, gh_in, loss_ref, g1_ref, g2_ref, gh_ref):
+    heads, channels, bin_width = gh_ref.shape
     for k in range(heads):
-        c, kk = divmod(k, half_heads)
-        gh_ref[k] = jnp.transpose(gh.out[c, :, kk].astype(F32).reshape(bin_width, channels))
-    g2.step5()
-    unpack_grad(g2.out, g2_ref, channels)
-    whole = jnp.sum(g2.out[1, 0, 4].astype(F32), axis=0, keepdims=True)
-    loss_ref[...] = jnp.sum(whole, axis=1, keepdims=True) * (1.0 / (heads * cells_all))
-    g1.step4()
-    g1.step5()
-    unpack_grad(g1.out, g1_ref, channels)
+        c, kk = divmod(k, heads // 2)
+        gh_ref[k] = jnp.transpose(gh_in[c, :, kk].astype(F32).reshape(bin_width, channels))
+    unpack_grad(g2_in, g2_ref, channels)
+    unpack_grad(g1_in, g1_ref, channels)
+    whole = jnp.sum(g2_in[1, 0, 4].astype(F32), axis=0, keepdims=True)
+    loss_ref[...] = jnp.sum(whole, axis=1, keepdims=True) * (1.0 / count)
 
 
 def per_device(inputs, conv_one, conv_two, head_weight, targets):
@@ -537,21 +625,30 @@
     cells_all = rows * lat * bins * width * lon
     scratch = plan(lat, lon, bins, rows, width, channels, heads, bin_width)
     vmem = pl.BlockSpec(memory_space=pltpu.VMEM)
+    hbm = pl.BlockSpec(memory_space=pl.ANY)
+    parts = pl.pallas_call(
+        functools.partial(kernel, (lat, lon, bins, cells_all), tuple(scratch)),
+        out_shape=[
+            jax.ShapeDtypeStruct(scratch[name + "_out"].shape, BF) for name in ("g1", "g2", "gh")
+        ],
+        in_specs=[hbm] * 5,
+        out_specs=[hbm] * 3,
+        scratch_shapes=list(scratch.values()),
+        compiler_params=pltpu.CompilerParams(
+            collective_id=0, has_side_effects=True, vmem_limit_bytes=60 << 20
+        ),
+    )(inputs, conv_one, conv_two, head_weight, targets)
     loss, g1, g2, gh = pl.pallas_call(
-        functools.partial(kernel, (lat, lon, bins, cells_all), tuple(scratch)),
+        functools.partial(unpack, heads * cells_all),
         out_shape=[
             jax.ShapeDtypeStruct((1, 1), F32),
             jax.ShapeDtypeStruct(conv_one.shape, F32),
             jax.ShapeDtypeStruct(conv_two.shape, F32),
             jax.ShapeDtypeStruct(head_weight.shape, F32),
         ],
-        in_specs=[vmem] * 5,
+        in_specs=[vmem] * 3,
         out_specs=[vmem] * 4,
-        scratch_shapes=list(scratch.values()),
-        compiler_params=pltpu.CompilerParams(
-            collective_id=0, has_side_effects=True, vmem_limit_bytes=56 << 20
-        ),
-    )(inputs, conv_one, conv_two, head_weight, targets)
+    )(*parts)
     return (loss.reshape(()), g1, g2, gh)
 
 

time: 89.1 us -> 77.1 us (0.87)
  Pallas kernels: 82.8 us -> 76.3 us
  local copies, waits for them, and re-layouts: 3.78 us -> 0 us
  between operations: 2.4 us -> 0.64 us
    pallas_call x1, Pallas kernels: 82.8 us -> 74 us  [per_device(): pl.pallas_call(functools.partial(kernel, (lat, lon, bins, cells_all), tup...]
    unnamed x7 -> x0, local copies, waits for them, and re-layouts: 3.78 us -> none
    pallas_call x0 -> x1, Pallas kernels: none -> 2.3 us  [per_device(): pl.pallas_call(functools.partial(unpack, heads * cells_all), out_shape=[j...]
where the time goes in v2:
time: 77.1 us; the launch traced here: 77 us
  Pallas kernels  76.3 us (99%)
    pallas_call x1, Pallas kernels, per_device(): pl.pallas_call(functools.partial(kernel, (lat, lon, bins, cells_all), tup...  74 us
    pallas_call x1, Pallas kernels, per_device(): pl.pallas_call(functools.partial(unpack, heads * cells_all), out_shape=[j...  2.3 us

profile of v2, /device:TPU:1, one launch (start us, length us, event | category | flops | bytes accessed | tf_op | source)
XLA Modules:
  0.0 77.0 jit_solution(7114995771975412414)
XLA Ops:
  0.6 74.0 %shard_map.84 = (bf16[2,16,5,8,128]{4,3,2,1,0:T(8,128)(2,1)}, bf16[2,16,5,8,128]{4,3,2,1,0:T(8,128)(2,1)}, bf16[2,16,2,8,128]{4,3,2,1,0:T(8,128)(2,1)}) custom-call(bf16[8,256,128]{2,1,0:T(8,128)(2,1)} %x_ref.1, bf16[3,3,128,128]{3,2,1,0:T(8,128)(2,1)} %w1_ref.1, bf16[3,3,128,128]{3,2,1,0:T(8,128)(2,1)} %w2_ref.1, bf16[4,128,128]{2,1,0:T(8,128)(2,1)} %hw_ref.1, ...), custom_call_target="tpu_custom_call" | custom-call | tf_op jit(solution)/shard_map/pallas_call | solution.py:629
  74.7 2.3 %shard_map.85 = (f32[1,1]{1,0:T(1,128)}, f32[3,3,128,128]{3,2,1,0:T(8,128)}, f32[3,3,128,128]{3,2,1,0:T(8,128)}, f32[4,128,128]{2,1,0:T(8,128)}) custom-call(bf16[2,16,5,8,128]{4,3,2,1,0:T(8,128)(2,1)} %get-tuple-element.11.g1_in, bf16[2,16,5,8,128]{4,3,2,1,0:T(8,128)(2,1)} %get-tuple-element.12.g2_in, bf16[2,16,2,8,128]{4,3,2,1,0:T(8,128)(2,1)} %get-tuple-element.13.gh_in), custom_call_target="tpu_custom_call" | custom-call | tf_op jit(solution)/shard_map/pallas_call | solution.py:641

commit v3 on v2

--- a/solution.py
+++ b/solution.py
@@ -56,25 +56,26 @@
         load=dma((5,)),
         store=dma((6,)),
         loss_acc=vm((1, width), F32),
+        act_turned=vm((rows, channels, width), BF),
+        back_acc=vm((rows, channels, width), F32),
         g_acc=vm((3 * channels, 3 * channels), F32),
-        col_out=vm((3, 2, 2, rows, channels), F32),
-        col_in=vm((3, 2, 3, rows, channels), F32),
+        col_out=vm((3, 3, 2, rows, channels), F32),
+        col_in=vm((3, 2, 4, rows, channels), F32),
         row_in=vm((3, 2, width, channels), BF),
-        halo_send=dma((3, 8)),
-        halo_recv=dma((3, 8)),
-        hw_send=dma((2, bins)),
-        hw_recv=dma((2, bins)),
+        halo_send=dma((3, 10)),
+        halo_recv=dma((3, 10)),
+        hw_send=dma((2, 2, bins)),
+        hw_recv=dma((2, 2, bins)),
     )
-    shapes = dict(gh=((bins, heads // 2), (heads // 2,)), g2=((5,), (5,)), g1=((5,), (5,)))
-    for name, (first, second) in shapes.items():
+    for name, (first, second) in dict(early=(2 * bins + 5, 7), late=(5, 5)).items():
         tile = (qr, channels)
-        s[name + "_part"] = vm((2, nq) + first + tile, BF)
-        s[name + "_core"] = vm((nq,) + first + tile, BF)
-        s[name + "_half"] = vm((nq,) + first + tile, BF)
-        s[name + "_plane"] = vm((nq,) + first + tile, BF)
-        s[name + "_sum"] = vm(first + tile, BF)
-        s[name + "_ring"] = vm((nz,) + second + tile, BF)
-        s[name + "_out"] = vm((2, nq) + second + tile, BF)
+        s[name + "_part"] = vm((2, nq, first) + tile, BF)
+        s[name + "_core"] = vm((nq, first) + tile, BF)
+        s[name + "_half"] = vm((nq, first) + tile, BF)
+        s[name + "_plane"] = vm((nq, first) + tile, BF)
+        s[name + "_sum"] = vm((bins, second) + tile, BF)
+        s[name + "_ring"] = vm((nz, second) + tile, BF)
+        s[name + "_out"] = vm((2, nq, second) + tile, BF)
         s[name + "_send"] = dma((2 + 2 * nq + nz,))
         s[name + "_recv"] = dma((2 + 2 * nq + nz,))
     return s
@@ -122,8 +123,17 @@
             yield dz, zhi, self.device(lat=self.at(zlo=zlo), bin=zhi)
 
     def bins(self):
-        for db in range(1, self.bin_size):
-            yield db, self.device(bin=(self.bin + db) % self.bin_size)
+        if self.nzl == 2 and self.bin_size == 4:
+            side = 2 * self.zlo - 1
+            for step, other in ((1, True), (2, True), (1, False)):
+                zlo = 1 - self.zlo if other else self.zlo
+                to = (self.bin + step * side + 4) % 4
+                source = (self.bin + (step if other else -step) * side + 4) % 4
+                yield source, self.device(lat=self.at(zlo=zlo), bin=to)
+        else:
+            for step in range(1, self.bin_size):
+                to = (self.bin + step) % self.bin_size
+                yield (self.bin - step + self.bin_size) % self.bin_size, self.device(bin=to)
 
     def neighbour(self, down, right):
         block = (self.row_block + down) % self.row_blocks
@@ -133,6 +143,7 @@
 
 
 NEIGHBOURS = [(-1, 0), (1, 0), (0, -1), (0, 1), (-1, -1), (-1, 1), (1, -1), (1, 1)]
+EARLY = (8, 9)
 
 
 def enter(place):
@@ -171,7 +182,7 @@
     def go(self, i, src, dst):
         k, s = self.k, self.s
         self.copies[i] = remote(
-            src, dst, s["halo_send"].at[k, i], s["halo_recv"].at[k, i], self.place.neighbour(*NEIGHBOURS[i])
+            src, dst, s["halo_send"].at[k, i], s["halo_recv"].at[k, i], self.place.neighbour(*NEIGHBOURS[i - 6 if i in EARLY else i])
         )
 
     def send_rows(self, top, bottom):
@@ -183,22 +194,25 @@
         s["col_out"][k, which, 0] = frame[self.column(0), :]
         s["col_out"][k, which, 1] = frame[self.column(self.width - 1), :]
         for i in use:
-            down, right = NEIGHBOURS[i]
+            down, right = NEIGHBOURS[i - 6 if i in EARLY else i]
             src = s["col_out"].at[k, which, 0 if right < 0 else 1]
-            self.go(i, src, s["col_in"].at[k, 1 if right < 0 else 0, 1 - down])
+            self.go(i, src, s["col_in"].at[k, 1 if right < 0 else 0, 3 if i in EARLY else 1 - down])
 
     def send_sides(self):
         self.send_columns(0, (2, 3))
 
+    def send_early_sides(self):
+        self.send_columns(2, EARLY)
+
     def send_corners(self):
         self.send_columns(1, (4, 5, 6, 7))
 
-    def receive_sides(self):
+    def receive_sides(self, early=False):
         k, place, s, frame = self.k, self.place, self.s, self.s["frame"]
-        for i in (2, 3):
+        for i in EARLY if early else (2, 3):
             self.copies[i].wait()
         for side, there, c in ((0, place.lon > 0, -1), (1, place.lon < place.lon_size - 1, self.width)):
-            frame[self.column(c), :] = jnp.where(there, s["col_in"][k, side, 1], 0.0)
+            frame[self.column(c), :] = jnp.where(there, s["col_in"][k, side, 3 if early else 1], 0.0)
 
     def receive_rest(self):
         k, place, s, frame = self.k, self.place, self.s, self.s["frame"]
@@ -233,9 +247,9 @@
     lax.fori_loop(0, count, body, 0)
 
 
-def fix_patches(frame, patches, rows, width):
+def fix_patches(frame, patches, lines, width):
     pitch = width + 16
-    for r in range(1, rows + 1):
+    for r in lines:
         patches[pl.ds(r * width, 16), :128] = frame[pl.ds(r * pitch + 7, 16), :].astype(BF)
         patches[pl.ds((r + 1) * width - 16, 16), 256:] = frame[
             pl.ds(r * pitch + width - 7, 16), :
@@ -312,8 +326,8 @@
 
 
 class Reduce:
-    def __init__(self, name, place, s, spread, extra=False):
-        self.place, self.spread, self.extra = place, spread, extra
+    def __init__(self, name, place, s, heads=0):
+        self.place, self.heads = place, heads
         for part in ("part", "core", "half", "plane", "sum", "ring", "out", "send", "recv"):
             setattr(self, part, s[name + "_" + part])
         self.sems = 0
@@ -322,10 +336,10 @@
         return remote(src, dst, self.send.at[i], self.recv.at[i], device)
 
     def rounded(self, value):
-        if not self.extra:
+        if not self.heads:
             return value.astype(BF)
-        last = jnp.where(self.place.core == 1, joined(value[4]), value[4])
-        return jnp.concatenate([value[:4], last[None]], axis=0).astype(BF)
+        last = jnp.where(self.place.core == 1, joined(value[-1]), value[-1])
+        return jnp.concatenate([value[:-1], last[None]], axis=0).astype(BF)
 
     def step0(self):
         p = self.place
@@ -353,13 +367,17 @@
         value = self.half[p.q].astype(F32)
         for d in range(1, p.nq):
             value = value + self.plane[d].astype(F32)
-        self.sum[...] = self.rounded(value)
-        if self.spread:
-            self.ring[p.z] = self.sum[p.bin]
+        value = self.rounded(value)
+        if self.heads:
+            for b in range(p.bin_size):
+                own = value[2 * b : 2 * b + 2]
+                self.sum[b] = jnp.concatenate([own, value[self.heads :]], axis=0)
         else:
-            self.ring[p.z] = self.sum[...]
+            self.sum[0] = value
+        mine = p.bin if self.heads else 0
+        self.ring[p.z] = self.sum[mine]
         self.copies = [
-            self.go(self.sum.at[zhi] if self.spread else self.sum, self.ring.at[p.z], 1 + p.nq + dz, device)
+            self.go(self.sum.at[zhi if self.heads else 0], self.ring.at[p.z], 1 + p.nq + dz, device)
             for dz, zhi, device in p.ring()
         ]
 
@@ -387,20 +405,20 @@
             copy.wait()
 
 
-def pack_grad(acc, part, channels):
+def pack_grad(acc, part, channels, first=0):
     qr = part.shape[-2]
     for a in range(3):
         for b in range(3):
             c, t = divmod(3 * a + b, 5)
             tap = acc[b * channels : (b + 1) * channels, a * channels : (a + 1) * channels]
-            part[c, :, t] = tap.reshape(channels // qr, qr, channels).astype(BF)
-
-
-def unpack_grad(out, result, channels):
+            part[c, :, first + t] = tap.reshape(channels // qr, qr, channels).astype(BF)
+
+
+def unpack_grad(out, result, channels, first=0):
     for a in range(3):
         for b in range(3):
             c, t = divmod(3 * a + b, 5)
-            result[a, b] = out[c, :, t].astype(F32).reshape(channels, channels)
+            result[a, b] = out[c, :, first + t].astype(F32).reshape(channels, channels)
 
 
 def turned(tile):
@@ -413,7 +431,7 @@
     return copy
 
 
-def kernel(sizes, names, x_ref, w1_ref, w2_ref, hw_ref, tg_ref, g1_ref, g2_ref, gh_ref, *refs):
+def kernel(sizes, names, x_ref, w1_ref, w2_ref, hw_ref, tg_ref, late_ref, early_ref, *refs):
     lat, lon, bins, cells_all = sizes
     s = dict(zip(names, refs))
     place = Place(lat, lon, bins)
@@ -435,29 +453,49 @@
     pl.semaphore_wait(pltpu.get_barrier_semaphore(), peers)
 
     halo = Halo(0, place, s)
-    my_heads = pl.ds(place.core * half_heads, half_heads)
-    hw_copies = [
-        remote(
-            hw_ref.at[my_heads],
-            hw_all.at[place.bin, my_heads],
-            s["hw_send"].at[0, db],
-            s["hw_recv"].at[0, db],
-            device,
-        )
-        for db, device in place.bins()
-    ]
+    own_first = place.core * half_heads
+    hw_copies = [[], []]
+    sources = [source for source, _ in place.bins()]
+
+    def send_head(kk):
+        k = own_first + kk
+        for j, (_, device) in enumerate(place.bins()):
+            hw_copies[kk].append(
+                remote(
+                    hw_ref.at[k],
+                    hw_all.at[place.bin, k],
+                    s["hw_send"].at[0, kk, j],
+                    s["hw_recv"].at[0, kk, j],
+                    device,
+                )
+            )
+
+    forwards = [[], []]
+
+    def forward_head(kk):
+        for j, source in enumerate(sources):
+            hw_copies[kk][j].wait()
+            there = hw_all.at[source, own_first + kk]
+            forwards[kk].append(
+                remote(
+                    there, there, s["hw_send"].at[1, kk, j], s["hw_recv"].at[1, kk, j], place.partner()
+                )
+            )
+
+    send_head(0)
     halo.send_rows(x_ref.at[0], x_ref.at[rows - 1])
     loads[0].wait()
     for r in range(rows):
         frame[halo.line(r), :] = s["x"][r].astype(F32)
     halo.send_sides()
     halo.send_corners()
+    send_head(1)
 
     fill_patches(frame, s["px"], 1, rows, 1, width)
     loads[1].wait()
     fill_weights(s["w_one"], lambda a, b: s["w1"][a, b], channels)
     halo.receive_sides()
-    fix_patches(frame, s["px"], rows, width)
+    fix_patches(frame, s["px"], range(1, rows + 1), width)
 
     def finish_one(r, value):
         s["pre_one"][r] = value
@@ -466,10 +504,12 @@
         frame[halo.line(r), :] = act.astype(F32)
 
     convolve(s["px"], s["w_one"], 1, (rows - 2) // 2, 2, width, finish_one)
+    next_halo = Halo(1, place, s)
+    next_halo.send_early_sides()
     halo.receive_rest()
     fill_patches(frame, s["px"], 0, 2, rows + 1, width)
     convolve_outer(s["px"], s["w_one"], rows, width, finish_one)
-    halo = Halo(1, place, s)
+    halo = next_halo
     halo.send_sides()
     halo.send_rows(s["act_one"].at[0], s["act_one"].at[rows - 1])
     halo.send_corners()
@@ -477,87 +517,114 @@
     fill_patches(frame, s["pa"], 1, rows, 1, width)
     loads[2].wait()
     fill_weights(s["w_two"], lambda a, b: s["w2"][a, b], channels)
-    for copy in hw_copies:
-        copy.wait()
-    hw_copies = []
-    for db in range(1, bins):
-        there = hw_all.at[(place.bin + db) % bins, my_heads]
-        hw_copies.append(
-            remote(there, there, s["hw_send"].at[1, db], s["hw_recv"].at[1, db], place.partner())
-        )
-    halo.receive_sides()
-    fix_patches(frame, s["pa"], rows, width)
+    fill_weights(s["w_flip"], lambda a, b: turned(s["w2"][2 - a, 2 - b]), channels)
+    halo.receive_sides(early=True)
+    fix_patches(frame, s["pa"], range(1, rows + 1), width)
 
     def finish_two(r, value):
         s["pre_two"][r] = value
-        s["act_two"][r] = jnp.maximum(value, 0.0).astype(BF)
+        act = jnp.maximum(value, 0.0).astype(BF)
+        s["act_two"][r] = act
+        s["act_turned"][r] = turned(act)
 
     convolve(s["pa"], s["w_two"], 2, (rows - 4) // 2, 2, width, finish_two)
 
-    for copy in loads[3:] + hw_copies:
+    for copy in loads[3:]:
         copy.wait()
-    hw_rows, hw_cols = s["hw_rows"], s["hw_cols"]
-    for b in range(bins):
-        for k in range(heads):
+    hw_rows, hw_cols, back_acc = s["hw_rows"], s["hw_cols"], s["back_acc"]
+    s["loss_acc"][...] = jnp.zeros_like(s["loss_acc"])
+    back_acc[...] = jnp.zeros_like(back_acc)
+    last_halo = Halo(2, place, s)
+
+    def prepare_head(k):
+        for b in range(bins):
             tile = hw_all[b, k]
             hw_cols[k, :, b * bin_width : (b + 1) * bin_width] = tile
             hw_rows[k, b * bin_width : (b + 1) * bin_width, :] = turned(tile)
-    s["loss_acc"][...] = jnp.zeros_like(s["loss_acc"])
-    last_halo = Halo(2, place, s)
-
-    def heads_body(i, carry):
-        r = (i + 2) % rows
-
-        feat_t = turned(s["act_two"][r])
-        back = jnp.zeros((channels, width), F32)
-        loss = s["loss_acc"][...]
+
+    def head_unit(k, pair):
         eight = lax.broadcasted_iota(jnp.int32, (8, width), 0)
         group = lax.broadcasted_iota(jnp.int32, (total // 8, 8, width), 0)
-        for k in range(heads):
-            logits = dot(hw_rows[k], feat_t).reshape(total // 8, 8, width)
-            highest = jnp.max(jnp.max(logits, axis=0), axis=0, keepdims=True)
-            raised = jnp.exp(logits - highest[None])
+        loss = s["loss_acc"][...]
+        logits = [dot(hw_rows[k], s["act_turned"][r]).reshape(total // 8, 8, width) for r in pair]
+        for r, value in zip(pair, logits):
+            highest = jnp.max(jnp.max(value, axis=0), axis=0, keepdims=True)
+            raised = jnp.exp(value - highest[None])
             summed = jnp.sum(jnp.sum(raised, axis=0), axis=0, keepdims=True)
             label = s["tg"][k, pl.ds(r, 1), :] - eight
             chosen = group * 8 == label[None]
-            picked = jnp.sum(jnp.sum(jnp.where(chosen, logits, 0.0), axis=0), axis=0, keepdims=True)
+            picked = jnp.sum(jnp.sum(jnp.where(chosen, value, 0.0), axis=0), axis=0, keepdims=True)
             loss = loss + (highest + jnp.log(summed) - picked)
-            value = raised * (scale / summed)[None]
-            grad = jnp.where(chosen, value - scale, value).reshape(total, width).astype(BF)
+            prob = raised * (scale / summed)[None]
+            grad = jnp.where(chosen, prob - scale, prob).reshape(total, width).astype(BF)
+            s["head_grad"][r, k] = grad
+            back_acc[r] += dot(hw_cols[k], grad)
+        s["loss_acc"][...] = loss
+
+    def head_row(r):
+        eight = lax.broadcasted_iota(jnp.int32, (8, width), 0)
+        group = lax.broadcasted_iota(jnp.int32, (total // 8, 8, width), 0)
+        loss = s["loss_acc"][...]
+        back = jnp.zeros((channels, width), F32)
+        for k in range(heads):
+            value = dot(hw_rows[k], s["act_turned"][r]).reshape(total // 8, 8, width)
+            highest = jnp.max(jnp.max(value, axis=0), axis=0, keepdims=True)
+            raised = jnp.exp(value - highest[None])
+            summed = jnp.sum(jnp.sum(raised, axis=0), axis=0, keepdims=True)
+            label = s["tg"][k, pl.ds(r, 1), :] - eight
+            chosen = group * 8 == label[None]
+            picked = jnp.sum(jnp.sum(jnp.where(chosen, value, 0.0), axis=0), axis=0, keepdims=True)
+            loss = loss + (highest + jnp.log(summed) - picked)
+            prob = raised * (scale / summed)[None]
+            grad = jnp.where(chosen, prob - scale, prob).reshape(total, width).astype(BF)
             s["head_grad"][r, k] = grad
             back = back + dot(hw_cols[k], grad)
         s["loss_acc"][...] = loss
-        hidden = jnp.where(s["pre_two"][r] > 0, jnp.transpose(back), 0.0).astype(BF)
+        back_acc[r] = back
+        finish_heads(r)
+
+    def finish_heads(r):
+        hidden = jnp.where(s["pre_two"][r] > 0, jnp.transpose(back_acc[r]), 0.0).astype(BF)
         s["back_two"][r + 1] = hidden
         frame[halo.line(r), :] = hidden.astype(F32)
-        return carry
-
-    lax.fori_loop(0, rows - 4, heads_body, 0)
+
+    def loop(count, body):
+        lax.fori_loop(0, count, lambda i, carry: (body(i), carry)[1], 0)
+
+    for kk in range(heads):
+        k = (own_first + kk) % heads
+        if kk < half_heads:
+            forward_head(kk)
+        else:
+            for copy in forwards[kk - half_heads]:
+                copy.wait()
+        prepare_head(k)
+        loop((rows - 4) // 2, lambda i: head_unit(k, (2 + 2 * i, 3 + 2 * i)))
+    loop(rows - 4, lambda i: finish_heads(2 + i))
+    halo.receive_sides()
+    fix_patches(frame, s["pa"], (1, rows), width)
     halo.receive_rest()
     fill_patches(frame, s["pa"], 0, 2, rows + 1, width)
     convolve(s["pa"], s["w_two"], 0, 2, rows - 2, width, finish_two)
-    lax.fori_loop(rows - 4, rows - 1, heads_body, 0)
+    loop(2, lambda i: head_row((rows - 1) * i))
     last_halo.send_rows(s["back_two"].at[1], s["back_two"].at[rows])
     last_halo.send_corners()
-    lax.fori_loop(rows - 1, rows, heads_body, 0)
+    loop(2, lambda i: head_row(1 + (rows - 3) * i))
     last_halo.send_sides()
     halo = last_halo
 
-    gh = Reduce("gh", place, s, True)
-    g2 = Reduce("g2", place, s, False, extra=True)
-    g1 = Reduce("g1", place, s, False)
-    qr = gh.part.shape[-2]
+    early = Reduce("early", place, s, heads=2 * bins)
+    late = Reduce("late", place, s)
+    qr = early.part.shape[-2]
     feats = s["act_two"][...].reshape(rows * width, channels)
     for k in range(heads):
         c, kk = divmod(k, half_heads)
         grads = jnp.concatenate([s["head_grad"][r, k] for r in range(rows)], axis=1)
         value = dot(grads, feats).reshape(bins, bin_width // qr, qr, channels)
         for b in range(bins):
-            gh.part[c, :, b, kk] = value[b].astype(BF)
-    gh.step0()
-
+            early.part[c, :, 2 * b + kk] = value[b].astype(BF)
     kernel_grad(s["pa"], s["back_two"], s["g_acc"], rows, width)
-    pack_grad(s["g_acc"], g2.part, channels)
+    pack_grad(s["g_acc"], early.part, channels, 2 * bins)
     loss = s["loss_acc"][...]
     lanes = loss[:, :128]
     for i in range(1, width // 128):
@@ -565,15 +632,14 @@
     row = lax.broadcasted_iota(jnp.int32, (qr, 128), 0)
     loss_tile = joined(jnp.where(row == 0, lanes, 0.0)).astype(BF)
     for q in range(place.nq):
-        g2.part[1, q, 4] = loss_tile
-        g1.part[1, q, 4] = jnp.zeros((qr, channels), BF)
-    g2.step0()
-
-    fill_weights(s["w_flip"], lambda a, b: turned(s["w2"][2 - a, 2 - b]), channels)
+        early.part[1, q, 2 * bins + 4] = loss_tile
+        late.part[1, q, 4] = jnp.zeros((qr, channels), BF)
+    early.step0()
+
     fill_patches(frame, s["pg"], 1, rows, 1, width)
-    gh.step1()
+    early.step1()
     halo.receive_sides()
-    fix_patches(frame, s["pg"], rows, width)
+    fix_patches(frame, s["pg"], range(1, rows + 1), width)
     halo.receive_rest()
     fill_patches(frame, s["pg"], 0, 2, rows + 1, width)
 
@@ -581,40 +647,34 @@
         s["back_one"][r + 1] = jnp.where(s["pre_one"][r] > 0, value, 0.0).astype(BF)
 
     convolve(s["pg"], s["w_flip"], 0, rows // 2, 2, width, finish_back)
-    g2.step1()
     kernel_grad(s["px"], s["back_one"], s["g_acc"], rows, width)
-    pack_grad(s["g_acc"], g1.part, channels)
-    g1.step0()
-    gh.step2()
-    g1.step1()
-    g2.step2()
-    gh.step3()
-    g1.step2()
-    g2.step3()
-    g1.step3()
-    gh.step4()
-    g2.step4()
-    gh.step5()
-    stores = [load(gh.out, gh_ref, s["store"].at[0])]
-    g2.step5()
-    stores.append(load(g2.out, g2_ref, s["store"].at[1]))
-    g1.step4()
-    stores.append(load(g1.out.at[place.core], g1_ref.at[place.core], s["store"].at[2]))
-    g1.step5()
+    pack_grad(s["g_acc"], late.part, channels)
+    late.step0()
+    late.step1()
+    early.step2()
+    late.step2()
+    early.step3()
+    late.step3()
+    early.step4()
+    early.step5()
+    stores = [load(early.out, early_ref, s["store"].at[0])]
+    late.step4()
+    stores.append(load(late.out.at[place.core], late_ref.at[place.core], s["store"].at[1]))
+    late.step5()
     other = 1 - place.core
-    stores.append(load(g1.out.at[other], g1_ref.at[other], s["store"].at[3]))
+    stores.append(load(late.out.at[other], late_ref.at[other], s["store"].at[2]))
     for copy in stores:
         copy.wait()
 
 
-def unpack(count, g1_in, g2_in, gh_in, loss_ref, g1_ref, g2_ref, gh_ref):
+def unpack(count, late_in, early_in, loss_ref, g1_ref, g2_ref, gh_ref):
     heads, channels, bin_width = gh_ref.shape
     for k in range(heads):
         c, kk = divmod(k, heads // 2)
-        gh_ref[k] = jnp.transpose(gh_in[c, :, kk].astype(F32).reshape(bin_width, channels))
-    unpack_grad(g2_in, g2_ref, channels)
-    unpack_grad(g1_in, g1_ref, channels)
-    whole = jnp.sum(g2_in[1, 0, 4].astype(F32), axis=0, keepdims=True)
+        gh_ref[k] = jnp.transpose(early_in[c, :, kk].astype(F32).reshape(bin_width, channels))
+    unpack_grad(early_in, g2_ref, channels, 2)
+    unpack_grad(late_in, g1_ref, channels)
+    whole = jnp.sum(early_in[1, 0, 6].astype(F32), axis=0, keepdims=True)
     loss_ref[...] = jnp.sum(whole, axis=1, keepdims=True) * (1.0 / count)
 
 
@@ -629,10 +689,10 @@
     parts = pl.pallas_call(
         functools.partial(kernel, (lat, lon, bins, cells_all), tuple(scratch)),
         out_shape=[
-            jax.ShapeDtypeStruct(scratch[name + "_out"].shape, BF) for name in ("g1", "g2", "gh")
+            jax.ShapeDtypeStruct(scratch[name + "_out"].shape, BF) for name in ("late", "early")
         ],
         in_specs=[hbm] * 5,
-        out_specs=[hbm] * 3,
+        out_specs=[hbm] * 2,
         scratch_shapes=list(scratch.values()),
         compiler_params=pltpu.CompilerParams(
             collective_id=0, has_side_effects=True, vmem_limit_bytes=60 << 20
@@ -646,7 +706,7 @@
             jax.ShapeDtypeStruct(conv_two.shape, F32),
             jax.ShapeDtypeStruct(head_weight.shape, F32),
         ],
-        in_specs=[vmem] * 3,
+        in_specs=[vmem] * 2,
         out_specs=[vmem] * 4,
     )(*parts)
     return (loss.reshape(()), g1, g2, gh)

time: 77.1 us -> 73.6 us (0.955)
  Pallas kernels: 76.3 us -> 72.9 us
    pallas_call x1, Pallas kernels: 74 us -> 70.5 us  [per_device(): pl.pallas_call(functools.partial(kernel, (lat, lon, bins, cells_all), tup...]
where the time goes in v3:
time: 73.6 us; the launch traced here: 73.5 us
  Pallas kernels  72.9 us (99%)
    pallas_call x1, Pallas kernels, per_device(): pl.pallas_call(functools.partial(kernel, (lat, lon, bins, cells_all), tup...  70.5 us
    pallas_call x1, Pallas kernels, per_device(): pl.pallas_call(functools.partial(unpack, heads * cells_all), out_shape=[j...  2.31 us

profile of v3, /device:TPU:1, one launch (start us, length us, event | category | flops | bytes accessed | tf_op | source)
XLA Modules:
  0.0 73.5 jit_solution(681166394168849232)
XLA Ops:
  0.6 70.5 %shard_map.84 = (bf16[2,16,5,8,128]{4,3,2,1,0:T(8,128)(2,1)}, bf16[2,16,7,8,128]{4,3,2,1,0:T(8,128)(2,1)}) custom-call(bf16[8,256,128]{2,1,0:T(8,128)(2,1)} %x_ref.1, bf16[3,3,128,128]{3,2,1,0:T(8,128)(2,1)} %w1_ref.1, bf16[3,3,128,128]{3,2,1,0:T(8,128)(2,1)} %w2_ref.1, bf16[4,128,128]{2,1,0:T(8,128)(2,1)} %hw_ref.1, s32[4,32,256]{2,1,0:T(8,128)} %tg_ref.1), custom_call_target="tpu_custom_call" | custom-call | tf_op jit(solution)/shard_map/pallas_call | solution.py:689
  71.2 2.3 %shard_map.85 = (f32[1,1]{1,0:T(1,128)}, f32[3,3,128,128]{3,2,1,0:T(8,128)}, f32[3,3,128,128]{3,2,1,0:T(8,128)}, f32[4,128,128]{2,1,0:T(8,128)}) custom-call(bf16[2,16,5,8,128]{4,3,2,1,0:T(8,128)(2,1)} %get-tuple-element.10.late_in, bf16[2,16,7,8,128]{4,3,2,1,0:T(8,128)(2,1)} %get-tuple-element.11.early_in), custom_call_target="tpu_custom_call" | custom-call | tf_op jit(solution)/shard_map/pallas_call | solution.py:701

commit v4 on v3

--- a/solution.py
+++ b/solution.py
@@ -47,7 +47,7 @@
         pre_two=vm((rows, width, channels), F32),
         hw_all=vm((bins, heads, channels, bin_width), BF),
         hw_rows=vm((heads, total, channels), BF),
-        hw_cols=vm((heads, channels, total), BF),
+        hw_cols=vm((channels, heads * total), BF),
         head_grad=vm((rows, heads, total, width), BF),
         x=vm((rows, width, channels), BF),
         w1=vm((3, 3, channels, channels), BF),
@@ -57,7 +57,6 @@
         store=dma((6,)),
         loss_acc=vm((1, width), F32),
         act_turned=vm((rows, channels, width), BF),
-        back_acc=vm((rows, channels, width), F32),
         g_acc=vm((3 * channels, 3 * channels), F32),
         col_out=vm((3, 3, 2, rows, channels), F32),
         col_in=vm((3, 2, 4, rows, channels), F32),
@@ -350,15 +349,14 @@
         for copy in self.copies:
             copy.wait()
 
-        def body(i, carry):
-            value = self.part[p.core, i].astype(F32) + self.core[i].astype(F32)
-            self.half[i] = self.rounded(value)
-            return carry
-
-        lax.fori_loop(0, p.nq, body, 0)
-        self.copies = [
-            self.go(self.half.at[q], self.plane.at[d], 1 + d, device) for d, q, device in p.plane()
-        ]
+        def add(q):
+            self.half[q] = self.rounded(self.part[p.core, q].astype(F32) + self.core[q].astype(F32))
+
+        self.copies = []
+        for d, q, device in p.plane():
+            add(q)
+            self.copies.append(self.go(self.half.at[q], self.plane.at[d], 1 + d, device))
+        add(p.q)
 
     def step2(self):
         p = self.place
@@ -506,6 +504,9 @@
     convolve(s["px"], s["w_one"], 1, (rows - 2) // 2, 2, width, finish_one)
     next_halo = Halo(1, place, s)
     next_halo.send_early_sides()
+    loads[2].wait()
+    fill_weights(s["w_two"], lambda a, b: s["w2"][a, b], channels)
+    fill_weights(s["w_flip"], lambda a, b: turned(s["w2"][2 - a, 2 - b]), channels)
     halo.receive_rest()
     fill_patches(frame, s["px"], 0, 2, rows + 1, width)
     convolve_outer(s["px"], s["w_one"], rows, width, finish_one)
@@ -515,9 +516,6 @@
     halo.send_corners()
 
     fill_patches(frame, s["pa"], 1, rows, 1, width)
-    loads[2].wait()
-    fill_weights(s["w_two"], lambda a, b: s["w2"][a, b], channels)
-    fill_weights(s["w_flip"], lambda a, b: turned(s["w2"][2 - a, 2 - b]), channels)
     halo.receive_sides(early=True)
     fix_patches(frame, s["pa"], range(1, rows + 1), width)
 
@@ -531,15 +529,15 @@
 
     for copy in loads[3:]:
         copy.wait()
-    hw_rows, hw_cols, back_acc = s["hw_rows"], s["hw_cols"], s["back_acc"]
+    hw_rows, hw_cols = s["hw_rows"], s["hw_cols"]
     s["loss_acc"][...] = jnp.zeros_like(s["loss_acc"])
-    back_acc[...] = jnp.zeros_like(back_acc)
     last_halo = Halo(2, place, s)
 
     def prepare_head(k):
         for b in range(bins):
             tile = hw_all[b, k]
-            hw_cols[k, :, b * bin_width : (b + 1) * bin_width] = tile
+            start = k * total + b * bin_width
+            hw_cols[:, pl.ds(pl.multiple_of(start, 128), bin_width)] = tile
             hw_rows[k, b * bin_width : (b + 1) * bin_width, :] = turned(tile)
 
     def head_unit(k, pair):
@@ -558,7 +556,6 @@
             prob = raised * (scale / summed)[None]
             grad = jnp.where(chosen, prob - scale, prob).reshape(total, width).astype(BF)
             s["head_grad"][r, k] = grad
-            back_acc[r] += dot(hw_cols[k], grad)
         s["loss_acc"][...] = loss
 
     def head_row(r):
@@ -578,13 +575,12 @@
             prob = raised * (scale / summed)[None]
             grad = jnp.where(chosen, prob - scale, prob).reshape(total, width).astype(BF)
             s["head_grad"][r, k] = grad
-            back = back + dot(hw_cols[k], grad)
+            back = back + dot(hw_cols[:, k * total : (k + 1) * total], grad)
         s["loss_acc"][...] = loss
-        back_acc[r] = back
-        finish_heads(r)
-
-    def finish_heads(r):
-        hidden = jnp.where(s["pre_two"][r] > 0, jnp.transpose(back_acc[r]), 0.0).astype(BF)
+        finish_heads(r, back)
+
+    def finish_heads(r, back):
+        hidden = jnp.where(s["pre_two"][r] > 0, jnp.transpose(back), 0.0).astype(BF)
         s["back_two"][r + 1] = hidden
         frame[halo.line(r), :] = hidden.astype(F32)
 
@@ -600,7 +596,11 @@
                 copy.wait()
         prepare_head(k)
         loop((rows - 4) // 2, lambda i: head_unit(k, (2 + 2 * i, 3 + 2 * i)))
-    loop(rows - 4, lambda i: finish_heads(2 + i))
+    def finish_inner(r):
+        grads = s["head_grad"][r].reshape(heads * total, width)
+        finish_heads(r, dot(hw_cols[...], grads))
+
+    loop(rows - 4, lambda i: finish_inner(2 + i))
     halo.receive_sides()
     fix_patches(frame, s["pa"], (1, rows), width)
     halo.receive_rest()
@@ -637,7 +637,6 @@
     early.step0()
 
     fill_patches(frame, s["pg"], 1, rows, 1, width)
-    early.step1()
     halo.receive_sides()
     fix_patches(frame, s["pg"], range(1, rows + 1), width)
     halo.receive_rest()
@@ -647,6 +646,7 @@
         s["back_one"][r + 1] = jnp.where(s["pre_one"][r] > 0, value, 0.0).astype(BF)
 
     convolve(s["pg"], s["w_flip"], 0, rows // 2, 2, width, finish_back)
+    early.step1()
     kernel_grad(s["px"], s["back_one"], s["g_acc"], rows, width)
     pack_grad(s["g_acc"], late.part, channels)
     late.step0()
@@ -667,15 +667,24 @@
         copy.wait()
 
 
-def unpack(count, late_in, early_in, loss_ref, g1_ref, g2_ref, gh_ref):
-    heads, channels, bin_width = gh_ref.shape
+def unpack(count, late_hbm, early_hbm, loss_ref, g1_hbm, g2_hbm, gh_hbm, *scratch):
+    late_in, early_in, g1, g2, gh, sems = scratch
+    heads, channels, bin_width = gh.shape
+    loads = [load(early_hbm, early_in, sems.at[0]), load(late_hbm, late_in, sems.at[1])]
+    loads[0].wait()
+    unpack_grad(early_in, g2, channels, 2)
+    stores = [load(g2, g2_hbm, sems.at[2])]
+    loads[1].wait()
+    unpack_grad(late_in, g1, channels)
+    stores.append(load(g1, g1_hbm, sems.at[3]))
     for k in range(heads):
         c, kk = divmod(k, heads // 2)
-        gh_ref[k] = jnp.transpose(early_in[c, :, kk].astype(F32).reshape(bin_width, channels))
-    unpack_grad(early_in, g2_ref, channels, 2)
-    unpack_grad(late_in, g1_ref, channels)
+        gh[k] = jnp.transpose(early_in[c, :, kk].astype(F32).reshape(bin_width, channels))
+    stores.append(load(gh, gh_hbm, sems.at[4]))
     whole = jnp.sum(early_in[1, 0, 6].astype(F32), axis=0, keepdims=True)
     loss_ref[...] = jnp.sum(whole, axis=1, keepdims=True) * (1.0 / count)
+    for copy in stores:
+        copy.wait()
 
 
 def per_device(inputs, conv_one, conv_two, head_weight, targets):
@@ -706,8 +715,16 @@
             jax.ShapeDtypeStruct(conv_two.shape, F32),
             jax.ShapeDtypeStruct(head_weight.shape, F32),
         ],
-        in_specs=[vmem] * 2,
-        out_specs=[vmem] * 4,
+        in_specs=[hbm] * 2,
+        out_specs=[vmem] + [hbm] * 3,
+        scratch_shapes=[
+            pltpu.VMEM(scratch["late_out"].shape, BF),
+            pltpu.VMEM(scratch["early_out"].shape, BF),
+            pltpu.VMEM(conv_one.shape, F32),
+            pltpu.VMEM(conv_two.shape, F32),
+            pltpu.VMEM(head_weight.shape, F32),
+            pltpu.SemaphoreType.DMA((5,)),
+        ],
     )(*parts)
     return (loss.reshape(()), g1, g2, gh)
 

time: 73.6 us -> 72.3 us (0.982)
  Pallas kernels: 72.9 us -> 71.5 us
    pallas_call x1, Pallas kernels: 70.5 us -> 68.8 us  [per_device(): pl.pallas_call(functools.partial(kernel, (lat, lon, bins, cells_all), tup...]
where the time goes in v4:
time: 72.3 us; the launch traced here: 72.2 us
  Pallas kernels  71.5 us (99%)
    pallas_call x1, Pallas kernels, per_device(): pl.pallas_call(functools.partial(kernel, (lat, lon, bins, cells_all), tup...  68.8 us
    pallas_call x1, Pallas kernels, per_device(): pl.pallas_call(functools.partial(unpack, heads * cells_all), out_shape=[j...  2.7 us

profile of v4, /device:TPU:1, one launch (start us, length us, event | category | flops | bytes accessed | tf_op | source)
XLA Modules:
  0.0 72.2 jit_solution(1803199066488780942)
XLA Ops:
  0.6 68.8 %shard_map.84 = (bf16[2,16,5,8,128]{4,3,2,1,0:T(8,128)(2,1)}, bf16[2,16,7,8,128]{4,3,2,1,0:T(8,128)(2,1)}) custom-call(bf16[8,256,128]{2,1,0:T(8,128)(2,1)} %x_ref.1, bf16[3,3,128,128]{3,2,1,0:T(8,128)(2,1)} %w1_ref.1, bf16[3,3,128,128]{3,2,1,0:T(8,128)(2,1)} %w2_ref.1, bf16[4,128,128]{2,1,0:T(8,128)(2,1)} %hw_ref.1, s32[4,32,256]{2,1,0:T(8,128)} %tg_ref.1), custom_call_target="tpu_custom_call" | custom-call | tf_op jit(solution)/shard_map/pallas_call | solution.py:698
  69.5 2.7 %shard_map.85 = (f32[1,1]{1,0:T(1,128)}, f32[3,3,128,128]{3,2,1,0:T(8,128)}, f32[3,3,128,128]{3,2,1,0:T(8,128)}, f32[4,128,128]{2,1,0:T(8,128)}) custom-call(bf16[2,16,5,8,128]{4,3,2,1,0:T(8,128)(2,1)} %get-tuple-element.10.late_hbm, bf16[2,16,7,8,128]{4,3,2,1,0:T(8,128)(2,1)} %get-tuple-element.11.early_hbm), custom_call_target="tpu_custom_call" | custom-call | tf_op jit(solution)/shard_map/pallas_call | solution.py:710

commit v5 on v4

--- a/solution.py
+++ b/solution.py
@@ -480,14 +480,13 @@
                 )
             )
 
+    halo.send_rows(x_ref.at[0], x_ref.at[rows - 1])
     send_head(0)
-    halo.send_rows(x_ref.at[0], x_ref.at[rows - 1])
     loads[0].wait()
     for r in range(rows):
         frame[halo.line(r), :] = s["x"][r].astype(F32)
     halo.send_sides()
     halo.send_corners()
-    send_head(1)
 
     fill_patches(frame, s["px"], 1, rows, 1, width)
     loads[1].wait()
@@ -504,6 +503,7 @@
     convolve(s["px"], s["w_one"], 1, (rows - 2) // 2, 2, width, finish_one)
     next_halo = Halo(1, place, s)
     next_halo.send_early_sides()
+    send_head(1)
     loads[2].wait()
     fill_weights(s["w_two"], lambda a, b: s["w2"][a, b], channels)
     fill_weights(s["w_flip"], lambda a, b: turned(s["w2"][2 - a, 2 - b]), channels)

time: 72.3 us -> 72.2 us (level)
  no operation moved by 1% of the time
where the time goes in v5:
time: 72.2 us; the launch traced here: 72.1 us
  Pallas kernels  71.5 us (99%)
    pallas_call x1, Pallas kernels, per_device(): pl.pallas_call(functools.partial(kernel, (lat, lon, bins, cells_all), tup...  68.8 us
    pallas_call x1, Pallas kernels, per_device(): pl.pallas_call(functools.partial(unpack, heads * cells_all), out_shape=[j...  2.7 us

profile of v5, /device:TPU:1, one launch (start us, length us, event | category | flops | bytes accessed | tf_op | source)
XLA Modules:
  0.0 72.1 jit_solution(15544724301467947539)
XLA Ops:
  0.6 68.8 %shard_map.84 = (bf16[2,16,5,8,128]{4,3,2,1,0:T(8,128)(2,1)}, bf16[2,16,7,8,128]{4,3,2,1,0:T(8,128)(2,1)}) custom-call(bf16[8,256,128]{2,1,0:T(8,128)(2,1)} %x_ref.1, bf16[3,3,128,128]{3,2,1,0:T(8,128)(2,1)} %w1_ref.1, bf16[3,3,128,128]{3,2,1,0:T(8,128)(2,1)} %w2_ref.1, bf16[4,128,128]{2,1,0:T(8,128)(2,1)} %hw_ref.1, s32[4,32,256]{2,1,0:T(8,128)} %tg_ref.1), custom_call_target="tpu_custom_call" | custom-call | tf_op jit(solution)/shard_map/pallas_call | solution.py:698
  69.4 2.7 %shard_map.85 = (f32[1,1]{1,0:T(1,128)}, f32[3,3,128,128]{3,2,1,0:T(8,128)}, f32[3,3,128,128]{3,2,1,0:T(8,128)}, f32[4,128,128]{2,1,0:T(8,128)}) custom-call(bf16[2,16,5,8,128]{4,3,2,1,0:T(8,128)(2,1)} %get-tuple-element.10.late_hbm, bf16[2,16,7,8,128]{4,3,2,1,0:T(8,128)(2,1)} %get-tuple-element.11.early_hbm), custom_call_target="tpu_custom_call" | custom-call | tf_op jit(solution)/shard_map/pallas_call | solution.py:710
